TPU v7x, 32 devices: a whole 2x2x4 slice. The times are simulated.
32 devices in a mesh: groups: 2 (over x), seq: 16 (over z, y, core).
Axes of the slice: x: 2, y: 2, z: 4, core: 2. Of those that a mesh axis runs over, the one named last changes fastest.
Arguments:
- queries: bfloat16 [32, 32, 1024], P('seq', 'groups'), parts along dimension 1, may hold values from -1100 to 1100
- keys: bfloat16 [32, 32, 128], P('seq', 'groups'), parts along dimension 1, may hold values from -4 to 4
- values: bfloat16 [32, 32, 128], P('seq', 'groups'), parts along dimension 1, may hold values from -6 to 6
- cache_keys: bfloat16 [32, 2048, 128], P(('groups', 'seq')), parts along dimension 0, may hold values from -4 to 4
- cache_values: bfloat16 [32, 2048, 128], P(('groups', 'seq')), parts along dimension 0, may hold values from -6 to 6
- cache_len: int32 [32, 16], P(None, 'groups'), parts along dimension 1, may hold values from 1 to 2048, as said below
- out_weight: bfloat16 [2048, 2048], P('seq'), may hold values from -0.5 to 0.5
- norm_gain: bfloat16 [2048], replicated, may hold values from 0.5 to 1.5
- expert_ids: int32 [32, 16, 8], P('seq', 'groups'), parts along dimension 1, may hold values from 0 to 31, all different within a row; in each aligned block of 16 rows (0 to 15, 16 to 31, ..., all dimensions but the last counted through in order) at most 5 rows name the same one
- route_weights: float32 [32, 16, 8], P('seq', 'groups'), parts along dimension 1, may hold values from 0.02 to 1
- w_gate: bfloat16 [32, 2048, 384], P('seq'), may hold values from -0.125 to 0.125
- w_up: bfloat16 [32, 2048, 384], P('seq'), may hold values from -0.125 to 0.125
- w_down: bfloat16 [32, 384, 2048], P('seq'), may hold values from -0.3125 to 0.3125
Outputs:
- projected: bfloat16 [32, 16, 2048], P('seq', 'groups'), parts along dimension 1
- moe_out: bfloat16 [32, 16, 2048], P('seq', 'groups'), parts along dimension 1
There are 2 independent parts, one for each index of `groups`. A program takes and returns all parts, laid end to end along the dimension named above; an argument that names none is the same for every part. Nothing has to cross between parts.
Inputs may be any that keep to these rules, and one draw needn't show every extreme that they name: `cache_len`: every new token sees at least one cached key; some token sees all 2048. `expert_ids`: rows are taken position-major over members; in each aligned block of 16 rows (the rows of one index of seq) no expert is named more than 5 times, a bound that some block reaches.
All inputs are finite; a program needn't handle non-finite values.
Results may differ from a plain program's by a relative error of at most 0.01.
Values may be sent and summed in bfloat16 or wider, within the bound.
No kernel may reach another device: no remote copies, remote signals or barrier semaphores. Data moves between devices by JAX's collectives and lax.ppermute only.
A program may use at most 64 MiB of HBM per device.

v0:
```python
import functools
import math

import jax
import jax.numpy as jnp
from jax import lax
from jax.experimental import pallas as pl
from jax.experimental.pallas import tpu as pltpu
from jax.sharding import PartitionSpec as P

D = 2048
HD = 128
TOPK = 8
QH = 16
KVH = 2
CAP = 5
LANES = 128

VMEM = pl.BlockSpec(memory_space=pltpu.VMEM)
SMEM = pl.BlockSpec(memory_space=pltpu.SMEM)
ANY = pl.BlockSpec(memory_space=pl.ANY)
HBM = pl.BlockSpec(memory_space=pltpu.HBM)


def iota(shape, dim):
    return lax.broadcasted_iota(jnp.int32, shape, dim)


def call(kernel, outs, args, scratch=(), far=(), loose=(), vmem_mib=12, flops=0, moved=0):
    return pl.pallas_call(
        kernel,
        out_shape=tuple(jax.ShapeDtypeStruct(s, d) for s, d in outs),
        in_specs=[
            SMEM if a.ndim == 1 else HBM if i in far else ANY if i in loose else VMEM
            for i, a in enumerate(args)
        ],
        out_specs=tuple(VMEM for _ in outs),
        scratch_shapes=list(scratch),
        compiler_params=pltpu.CompilerParams(vmem_limit_bytes=vmem_mib << 20),
        cost_estimate=pl.CostEstimate(flops=flops, bytes_accessed=moved, transcendentals=0),
    )(*(pltpu.with_memory_space_constraint(a, pltpu.HBM) if i in far else a for i, a in enumerate(args)))


def fetch(sources, targets, sems):
    copies = [
        pltpu.make_async_copy(source, target, sems.at[i])
        for i, (source, target) in enumerate(zip(sources, targets))
    ]
    for copy in copies:
        copy.start()
    return copies


def pack_kernel(
    query_hbm,
    key_hbm,
    value_hbm,
    id_hbm,
    share_hbm,
    out_ref,
    query_ref,
    key_ref,
    value_ref,
    id_ref,
    share_ref,
    sems,
):
    refs = (id_ref, share_ref, query_ref, key_ref, value_ref)
    for copy in fetch((id_hbm, share_hbm, query_hbm, key_hbm, value_hbm), refs, sems):
        copy.wait()
    per_rows, count, wide = query_ref.shape
    members = id_ref.shape[1]
    width = (out_ref.shape[2] - wide - 2 * HD) // 3
    lane = iota((members, width), 1)
    home = lane // TOPK == iota((members, width), 0)

    def flat(table):
        total = jnp.zeros((members, width), jnp.float32)
        for k in range(TOPK):
            total = jnp.where(home & (lane % TOPK == k), table[:, k : k + 1], total)
        row = jnp.sum(total, axis=0, keepdims=True)
        return jnp.broadcast_to(row, (count, width)).astype(jnp.bfloat16)

    for i in range(per_rows):
        out_ref[i, :, :wide] = query_ref[i]
        out_ref[i, :, wide : wide + HD] = key_ref[i]
        out_ref[i, :, wide + HD : wide + 2 * HD] = value_ref[i]
        share = share_ref[i]
        high = share.astype(jnp.bfloat16).astype(jnp.float32)
        at = wide + 2 * HD
        for table in (id_ref[i].astype(jnp.float32), high, share - high):
            out_ref[i, :, at : at + width] = flat(table)
            at += width


def split_kernel(at_ref, weight_hbm, *refs):
    parts, weight_ref, sems = refs[:-2], *refs[-2:]
    fetch((weight_hbm,), (weight_ref,), sems)[0].wait()
    chip = at_ref[0] // 2
    for k, part in enumerate(parts):
        for y in range(2):
            start = pl.multiple_of((chip ^ (2 * k + y)) * part.shape[2], LANES)
            part[y] = weight_ref[:, pl.ds(start, part.shape[2])]


def regroup_kernel(*refs):
    parts, (_, near_ref, far_ref) = refs[:-3], refs[-3:]
    for k, part in enumerate(parts):
        near_ref[k] = part[0]
        far_ref[k] = part[1]


def position_of(place, per_rows, core):
    return (place // per_rows * 2 + core) * per_rows + place % per_rows


def attend_kernel(
    per_rows,
    at_ref,
    row_ref,
    length_ref,
    key_hbm,
    value_hbm,
    keep_ref,
    send_ref,
    score_ref,
    key_ref,
    value_ref,
    sems,
):
    copies = fetch((key_hbm, value_hbm), (key_ref, value_ref), sems)
    new, heads = row_ref.shape[0], QH // KVH
    wide = heads * HD
    cached = key_ref.shape[0]
    step = math.gcd(cached, 512)
    member = at_ref[0] // KVH
    length = jnp.sum(
        jnp.where(iota(length_ref.shape, 1) == member, length_ref[...], 0).astype(jnp.float32),
        axis=1,
        keepdims=True,
    ).astype(jnp.int32)
    lengths = jnp.concatenate([length] * heads, axis=0)
    query = jnp.concatenate([row_ref[:, h * HD : (h + 1) * HD] for h in range(heads)], axis=0)
    rows = heads * new
    dims = (((1,), (1,)), ((), ()))
    fresh = lax.dot_general(
        query, row_ref[:, wide : wide + HD], dims, preferred_element_type=jnp.float32
    )
    causal = iota((new, new), 1) <= iota((new, new), 0)
    fresh = jnp.where(jnp.concatenate([causal] * heads, axis=0), fresh, -1e30)
    best = jnp.max(fresh, axis=1, keepdims=True)
    peak = jnp.full((rows, LANES), -1e30, jnp.float32)
    copies[0].wait()
    for at in range(0, cached, step):
        part = lax.dot_general(
            query, key_ref[at : at + step, :], dims, preferred_element_type=jnp.float32
        )
        part = jnp.where(iota((rows, step), 1) + at < lengths, part, -1e30)
        score_ref[:, at : at + step] = part
        for lane in range(0, step, LANES):
            peak = jnp.maximum(peak, part[:, lane : lane + LANES])
    best = jnp.maximum(best, jnp.max(peak, axis=1, keepdims=True))
    factor = HD ** (-0.5) * math.log2(math.e)
    fresh = jnp.exp2((fresh - best) * factor)
    sums = jnp.zeros((rows, LANES), jnp.float32)
    for at in range(0, cached, step):
        expo = jnp.exp2((score_ref[:, at : at + step] - best) * factor)
        score_ref[:, at : at + step] = expo
        for lane in range(0, step, LANES):
            sums = sums + expo[:, lane : lane + LANES]
    total = jnp.sum(fresh, axis=1, keepdims=True) + jnp.sum(sums, axis=1, keepdims=True)
    inverse = 1.0 / total
    result = jnp.dot(
        (fresh * inverse).astype(jnp.bfloat16),
        row_ref[:, wide + HD : wide + 2 * HD],
        preferred_element_type=jnp.float32,
    )
    copies[1].wait()
    for at in range(0, cached, step):
        result = result + jnp.dot(
            (score_ref[:, at : at + step] * inverse).astype(jnp.bfloat16),
            value_ref[at : at + step, :],
            preferred_element_type=jnp.float32,
        )
    result = result.astype(jnp.bfloat16)
    result = jnp.concatenate([result[h * new : (h + 1) * new] for h in range(heads)], axis=1)
    half = new // 2
    place = iota((new, new), 0)
    core = (at_ref[0] + place // half) % 2
    pick = iota((new, new), 1) == position_of(place % half, per_rows, core)
    result = jnp.dot(
        pick.astype(jnp.bfloat16), result, preferred_element_type=jnp.float32
    ).astype(jnp.bfloat16)
    keep_ref[...] = result[:half]
    send_ref[...] = result[half:]


def project_kernel(at_ref, rows_ref, *refs):
    columns, (out_ref, weight_ref) = refs[:-2], refs[-2:]
    me = at_ref[0]
    members, _, places, wide = rows_ref.shape
    rows = members * places
    owned = columns[0].shape[1]
    for i, ref in enumerate(columns):
        for k in range(ref.shape[0]):
            head = me ^ (4 * k + i)
            weight_ref[pl.ds(pl.multiple_of(head * owned, owned), owned), :] = ref[k]
    total = jnp.zeros(out_ref.shape, jnp.float32)
    for half in range(KVH):
        start = pl.multiple_of((me ^ half) % KVH * wide, wide)
        total = total + jnp.dot(
            rows_ref[:, half].reshape(rows, wide),
            weight_ref[pl.ds(start, wide), :],
            preferred_element_type=jnp.float32,
        )
    token = iota((rows, rows), 0)
    source = ((token % members) ^ (me // KVH)) * places + token // members
    pick = (iota((rows, rows), 1) == source).astype(jnp.bfloat16)
    out_ref[...] = jnp.dot(
        pick, total.astype(jnp.bfloat16), preferred_element_type=jnp.float32
    ).astype(jnp.bfloat16)


def expert_kernel(
    per_rows,
    at_ref,
    rows_ref,
    gain_ref,
    info_ref,
    gate_ref,
    up_ref,
    gate_peer_ref,
    up_peer_ref,
    down_hbm,
    down_peer_hbm,
    projected_ref,
    *refs,
):
    outs, (normed_ref, down_ref, down_peer_ref, sems) = refs[:-4], refs[-4:]
    copies = fetch((down_hbm, down_peer_hbm), (down_ref, down_peer_ref), sems)
    me = at_ref[0]
    chip, core = me // 2, me % 2
    chips, rows, lanes = rows_ref.shape
    new = info_ref.shape[0]
    per_dev = rows // chips
    members = per_dev // per_rows
    experts = gate_ref.shape[0]
    width = info_ref.shape[1] // 3

    squares = jnp.zeros((rows, lanes), jnp.float32)
    for i in range(chips):
        piece = rows_ref[i].astype(jnp.float32)
        squares = squares + piece * piece
    inverse = lax.rsqrt(jnp.sum(squares, axis=1, keepdims=True) / (chips * lanes) + 1e-06)
    own = pl.ds(pl.multiple_of(chip * per_dev, per_dev), per_dev)
    for i in range(chips):
        at = pl.ds(pl.multiple_of((chip ^ i) * lanes, lanes), lanes)
        gain = gain_ref[:, at].astype(jnp.float32)
        normed_ref[:, at] = (rows_ref[i].astype(jnp.float32) * inverse * gain).astype(jnp.bfloat16)
        projected_ref[:, at] = rows_ref[i, own, :]
    normed = jnp.concatenate(
        [
            normed_ref[pl.ds(pl.multiple_of((chip ^ i) * per_dev, per_dev), per_dev), :]
            for i in range(chips)
        ],
        axis=0,
    )

    def token(shape):
        r = iota(shape, 0)
        return ((r // per_dev) ^ chip) * per_dev + r % per_dev

    place = token((rows, new)) // members
    spread = iota((rows, new), 1) == position_of(place, per_rows, core)
    info = jnp.dot(
        spread.astype(jnp.bfloat16), info_ref[...], preferred_element_type=jnp.float32
    )
    mine = iota((rows, width), 1) // TOPK == token((rows, width)) % members
    share = jnp.where(mine, info[:, width : 2 * width] + info[:, 2 * width :], 0.0)
    whole = jnp.sum(share, axis=1, keepdims=True)
    hidden = []
    for device, gates, ups in ((me, gate_ref, up_ref), (me ^ 1, gate_peer_ref, up_peer_ref)):
        for e in range(experts):
            chosen = info[:, :width] == (device * experts + e).astype(jnp.float32)
            scale = jnp.sum(jnp.where(chosen, share, 0.0), axis=1, keepdims=True) / whole
            gate = jnp.dot(normed, gates[e], preferred_element_type=jnp.float32)
            up = jnp.dot(normed, ups[e], preferred_element_type=jnp.float32)
            hidden.append((gate / (1.0 + jnp.exp(-gate)) * up * scale).astype(jnp.bfloat16))
    for copy in copies:
        copy.wait()
    order = block_order(chips)
    step = 512
    for at in range(0, down_ref.shape[2], step):
        part = jnp.zeros((rows, step), jnp.float32)
        for e, value in enumerate(hidden):
            ref = (down_ref, down_peer_ref)[e // experts]
            part = part + jnp.dot(
                value, ref[e % experts, :, at : at + step], preferred_element_type=jnp.float32
            )
        part = part.astype(jnp.bfloat16)
        block = 0
        for out in outs:
            for i in range(out.shape[0]):
                where = order[block]
                out[i, :, at : at + step] = part[where * per_dev : (where + 1) * per_dev]
                block += 1


def block_order(chips):
    near = range(chips - 2, -1, -2)
    return [k + 1 for k in near] + list(near)


def add_kernel(near_ref, piece_ref, *outs):
    for i, out in enumerate(outs):
        out[...] = (
            near_ref[i].astype(jnp.float32) + piece_ref[i].astype(jnp.float32)
        ).astype(jnp.bfloat16)


def swap(value, offset):
    count = lax.axis_size("seq")
    return lax.ppermute(value, "seq", [(i, i ^ offset) for i in range(count)])


def scatter_pieces(far, near):
    pieces = []
    ahead = sum(part.shape[0] for part in near)
    for there, here in zip(far, near):
        shape = here.shape[1:]
        sums = call(
            add_kernel, [(shape, jnp.bfloat16)] * here.shape[0], (here, swap(there, 2))
        )
        for piece in sums:
            ahead -= 1
            pieces.append(swap(piece, 4 * ahead) if ahead else piece)
    return pieces


def gather_rows(own):
    count = lax.axis_size("seq")
    near = [own] + [swap(own, k) for k in range(count - 4, 0, -4)][::-1]
    far = [swap(piece, 2) for piece in near]
    return near, far


def interleave(near, far):
    return jnp.stack([p for pair in zip(near, far) for p in pair], axis=0)


def exchange_body(
    queries,
    keys,
    values,
    cache_keys,
    cache_values,
    cache_len,
    out_weight,
    norm_gain,
    expert_ids,
    route_weights,
    w_gate,
    w_up,
    w_down,
):
    count = lax.axis_size("seq")
    per_rows, members = queries.shape[0], count // KVH
    new = per_rows * count
    per_dev = per_rows * members
    rows = per_dev * count
    at = lax.axis_index("seq").astype(jnp.int32).reshape(1)
    width = -(-members * TOPK // LANES) * LANES
    wide = QH // KVH * HD
    bf16 = jnp.bfloat16
    (sent,) = call(
        pack_kernel,
        [((per_rows, count, wide + 2 * HD + 3 * width), bf16)],
        (queries, keys, values, expert_ids, route_weights),
        scratch=[
            pltpu.VMEM(a.shape, a.dtype)
            for a in (queries, keys, values, expert_ids, route_weights)
        ]
        + [pltpu.SemaphoreType.DMA((5,))],
        far=range(5),
    )
    taken = lax.all_to_all(sent, "seq", split_axis=1, concat_axis=0, tiled=True)
    taken = taken.reshape(new, sent.shape[2])
    owned = out_weight.shape[0]
    cached = cache_keys.shape[1]
    chips = count // 2
    lanes = D // chips
    gate_peer, up_peer, down_peer = swap(w_gate, 1), swap(w_up, 1), swap(w_down, 1)
    parts = call(
        split_kernel,
        [((2, owned, lanes), bf16)] * (chips // 2),
        (at, out_weight),
        scratch=[pltpu.VMEM(out_weight.shape, bf16), pltpu.SemaphoreType.DMA((1,))],
        far=(1,),
        moved=4 * out_weight.size,
    )
    parts = [parts[0]] + [swap(parts[k], 4 * k) for k in range(len(parts) - 1, 0, -1)][::-1]
    row_count = QH // KVH * new
    keep, send = call(
        functools.partial(attend_kernel, per_rows),
        [((new // 2, wide), bf16)] * 2,
        (at, taken, cache_len, cache_keys.reshape(cached, HD), cache_values.reshape(cached, HD)),
        scratch=[
            pltpu.VMEM((row_count, cached), jnp.float32),
            pltpu.VMEM((cached, HD), bf16),
            pltpu.VMEM((cached, HD), bf16),
            pltpu.SemaphoreType.DMA((2,)),
        ],
        far=(3, 4),
        flops=4 * row_count * cached * HD,
        moved=4 * cached * HD,
    )
    peer = swap(send, 1)
    own = jnp.stack([keep, peer])
    heads = interleave(*gather_rows(own))
    near, far = call(
        regroup_kernel,
        [((chips // 2, owned, lanes), bf16)] * 2,
        (*parts, own),
        loose=(len(parts),),
    )
    beyond = swap(far, 2)
    half = rows // 2
    (projected,) = call(
        project_kernel,
        [((half, lanes), bf16)],
        (at, heads, near, swap(near, 1), beyond, swap(beyond, 1)),
        scratch=[pltpu.VMEM((D, lanes), bf16)],
        flops=2 * half * D * lanes,
        moved=4 * half * D,
    )
    gathered = interleave(*gather_rows(projected))
    info = taken[:, wide + 2 * HD :]
    projected, *blocks = call(
        functools.partial(expert_kernel, per_rows),
        [((per_dev, D), bf16)] + [((2, per_dev, D), bf16)] * (chips // 2),
        (
            at,
            gathered,
            norm_gain.reshape(1, D),
            info,
            w_gate,
            w_up,
            gate_peer,
            up_peer,
            w_down,
            down_peer,
        ),
        scratch=[
            pltpu.VMEM((half, D), bf16),
            pltpu.VMEM(w_down.shape, bf16),
            pltpu.VMEM(w_down.shape, bf16),
            pltpu.SemaphoreType.DMA((2,)),
        ],
        far=(8, 9),
        vmem_mib=30,
        flops=12 * half * w_gate.size,
        moved=12 * w_gate.size,
    )
    pieces = scatter_pieces(blocks[: chips // 4], blocks[chips // 4 :])
    mixed = sum(piece.astype(jnp.float32) for piece in pieces)
    shape = (per_rows, members, D)
    return (projected.reshape(shape), mixed.astype(jnp.bfloat16).reshape(shape))


def fits(mesh, out_rows, positions, experts):
    count = mesh.shape["seq"]
    owned = out_rows // count
    per_dev = positions // count * (count // KVH)
    power = count & (count - 1) == 0 and count >= 8
    small = per_dev * count * D * 2 <= 2 << 20
    return power and owned == HD == LANES and count * LANES == D and per_dev % 16 == 0 and positions % 16 == 0 and small and experts <= 256


def attend(query_heads, key_rows, value_rows, lengths):
    new_count = query_heads.shape[0]
    cache_count = key_rows.shape[0] - new_count
    scores = jnp.einsum(
        "qhd,kd->hqk", query_heads, key_rows, preferred_element_type=jnp.float32
    ) * HD ** (-0.5)
    cached_ok = jnp.arange(cache_count, dtype=jnp.int32)[None, :] < lengths[:, None]
    causal_ok = (
        jnp.arange(new_count, dtype=jnp.int32)[None, :]
        <= jnp.arange(new_count, dtype=jnp.int32)[:, None]
    )
    visible = jnp.concatenate([cached_ok, causal_ok], axis=1)
    scores = jnp.where(visible[None], scores, -1e30)
    row_max = jnp.max(scores, axis=-1, keepdims=True)
    expo = jnp.exp(scores - row_max)
    row_sum = jnp.sum(expo, axis=-1, keepdims=True)
    weights = (expo / row_sum).astype(jnp.bfloat16)
    result = jnp.einsum("hqk,kd->qhd", weights, value_rows, preferred_element_type=jnp.float32)
    return result.astype(jnp.bfloat16).reshape(new_count, -1)


def plain_body(
    queries,
    keys,
    values,
    cache_keys,
    cache_values,
    cache_len,
    out_weight,
    norm_gain,
    expert_ids,
    route_weights,
    w_gate,
    w_up,
    w_down,
):
    slot_count = lax.axis_size("seq")
    per_rows = queries.shape[0]
    members = slot_count // KVH
    group_q = QH // KVH
    new_count = per_rows * slot_count
    position_index = lax.axis_index("seq")
    member = position_index // KVH
    query_rows, key_new, value_new = (
        lax.all_to_all(queries, "seq", split_axis=1, concat_axis=0, tiled=True),
        lax.all_to_all(keys, "seq", split_axis=1, concat_axis=0, tiled=True),
        lax.all_to_all(values, "seq", split_axis=1, concat_axis=0, tiled=True),
    )
    key_rows = jnp.concatenate([cache_keys[0], key_new.reshape(new_count, HD)], axis=0)
    value_rows = jnp.concatenate([cache_values[0], value_new.reshape(new_count, HD)], axis=0)
    lengths = lax.dynamic_slice_in_dim(cache_len, member, 1, 1)[:, 0]
    attended = attend(query_rows.reshape(new_count, group_q, HD), key_rows, value_rows, lengths)
    returned_heads = lax.all_to_all(
        attended[:, None, :], "seq", split_axis=0, concat_axis=1, tiled=True
    )
    token_heads = returned_heads.reshape(per_rows * members, QH * HD)
    projected_f = jnp.dot(
        token_heads,
        lax.all_gather(out_weight, "seq", axis=0, tiled=True),
        preferred_element_type=jnp.float32,
    )
    projected_f = projected_f.reshape(per_rows, members, D)
    projected = projected_f.astype(jnp.bfloat16)
    token_count = per_rows * members
    flat_rows = projected.reshape(token_count, D).astype(jnp.float32)
    stats = jnp.mean(flat_rows * flat_rows, axis=-1, keepdims=True)
    normed = (flat_rows * lax.rsqrt(stats + 1e-06) * norm_gain.astype(jnp.float32)).astype(
        jnp.bfloat16
    )
    exp_dev = w_gate.shape[0]
    expert_count = exp_dev * slot_count
    chosen_ids = expert_ids.reshape(token_count * TOPK)
    onehot = (chosen_ids[:, None] == jnp.arange(expert_count, dtype=jnp.int32)[None, :]).astype(
        jnp.int32
    )
    slot_rank = jnp.sum((jnp.cumsum(onehot, axis=0) - onehot) * onehot, axis=1)
    owner = chosen_ids // exp_dev
    local_expert = chosen_ids % exp_dev
    slot_target = (local_expert * slot_count + owner) * CAP + slot_rank
    total_slots = exp_dev * slot_count * CAP
    token_of = jnp.arange(token_count * TOPK, dtype=jnp.int32) // TOPK
    source_row = jnp.full((total_slots,), -1, jnp.int32).at[slot_target].set(token_of)
    filled = source_row >= 0
    outgoing = jnp.where(
        filled[:, None], normed[jnp.maximum(source_row, 0)], jnp.zeros((), jnp.bfloat16)
    )
    outgoing = outgoing.reshape(exp_dev, slot_count, CAP, D)
    incoming = lax.all_to_all(outgoing, "seq", split_axis=1, concat_axis=1, tiled=True)
    row_block = incoming.reshape(exp_dev, slot_count * CAP, D)
    gate_out = jnp.einsum("ecd,edf->ecf", row_block, w_gate, preferred_element_type=jnp.float32)
    up_out = jnp.einsum("ecd,edf->ecf", row_block, w_up, preferred_element_type=jnp.float32)
    hidden_act = (jax.nn.silu(gate_out) * up_out).astype(jnp.bfloat16)
    expert_out = jnp.einsum(
        "ecf,efd->ecd", hidden_act, w_down, preferred_element_type=jnp.float32
    ).astype(jnp.bfloat16)
    expert_back = lax.all_to_all(
        expert_out.reshape(exp_dev, slot_count, CAP, D),
        "seq",
        split_axis=1,
        concat_axis=1,
        tiled=True,
    )
    picked = expert_back.reshape(total_slots, D)[slot_target].reshape(token_count, TOPK, D)
    raw_weights = route_weights.reshape(token_count, TOPK)
    norm_weights = raw_weights / jnp.sum(raw_weights, axis=1, keepdims=True)
    mixed = jnp.sum(norm_weights[:, :, None] * picked.astype(jnp.float32), axis=1)
    moe_out = mixed.astype(jnp.bfloat16).reshape(per_rows, members, D)
    return (projected, moe_out)


def solution(mesh):
    def run(*args):
        exchanged = fits(mesh, args[6].shape[0], args[0].shape[0], args[10].shape[0])
        step = jax.shard_map(
            exchange_body if exchanged else plain_body,
            mesh=mesh,
            in_specs=(
                P("seq", "groups", None),
                P("seq", "groups", None),
                P("seq", "groups", None),
                P(("groups", "seq"), None, None),
                P(("groups", "seq"), None, None),
                P(None, "groups"),
                P("seq", None),
                P(),
                P("seq", "groups", None),
                P("seq", "groups", None),
                P("seq", None, None),
                P("seq", None, None),
                P("seq", None, None),
            ),
            out_specs=(P("seq", "groups", None), P("seq", "groups", None)),
            check_vma=False,
        )
        return step(*args)

    return run
```

profile of v0, /device:TPU:0, one launch (start us, length us, event | category | flops | bytes accessed | tf_op | source)
XLA Modules:
  0.0 103.1 jit_solution(12092871019868647170)
XLA Ops:
  2.4 7.4 %all-to-all-start = ((bf16[2,16,1664]{2,0,1:T(2,128)(2,1)}), bf16[2,16,1664]{2,0,1:T(2,128)(2,1)S(1)}, u32[]{:S(2)}, u32[]{:S(2)}) async-start(bf16[2,16,1664]{2,0,1:T(2,128)(2,1)} %copy.17), calls=%async_computation | async-start | bytes 212992 | tf_op jit(solution)/shard_map/all_to_all | solution.py:386
  10.6 6.7 %all-to-all-done = bf16[2,16,1664]{2,0,1:T(2,128)(2,1)S(1)} async-done(((bf16[2,16,1664]{2,0,1:T(2,128)(2,1)}), bf16[2,16,1664]{2,0,1:T(2,128)(2,1)S(1)}, u32[]{:S(2)}, u32[]{:S(2)}) %all-to-all-start) | async-done | bytes 106528 | tf_op jit(solution)/shard_map/all_to_all | solution.py:386
  17.4 2.7 %shard_map.141 = (bf16[16,1024]{1,0:T(8,128)(2,1)S(1)}, bf16[16,1024]{1,0:T(8,128)(2,1)S(1)}) custom-call(s32[1]{0:T(128)} %bitcast.at_ref, bf16[32,1664]{1,0:T(8,128)(2,1)S(1)} %reshape.27.row_ref, s32[32,8]{1,0:T(8,128)S(1)} %copy.18.length_ref, bf16[2048,128]{1,0:T(8,128)(2,1)} %bitcast.47, bf16[2048,128]{1,0:T(8,128)(2,1)} %bitcast.48), custom_call_target="tpu_custom_call" | custom-call | flops 268435456 | bytes 1048576 | tf_op jit(solution)/shard_map/pallas_call | solution.py:30
  22.8 3.0 %collective-permute-start.10 = (bf16[2,128,256]{2,1,0:T(8,128)(2,1)S(1)}, bf16[2,128,256]{2,1,0:T(8,128)(2,1)S(1)}, u32[]{:S(2)}, u32[]{:S(2)}) collective-permute-start(bf16[2,128,256]{2,1,0:T(8,128)(2,1)S(1)} %get-tuple-element.24), channel_id=1, source_target_pairs={{0,12},{1,13},{2,14},{3,15},{4,8},{5,9},{6,10},{7,11},{8,4},{9,5},... | collective-permute-start | bytes 393224 | tf_op jit(solution)/shard_map/ppermute | solution.py:323
  27.1 1.8 %collective-permute-done.8.refs_1_ = bf16[2,128,256]{2,1,0:T(8,128)(2,1)S(1)} collective-permute-done((bf16[2,128,256]{2,1,0:T(8,128)(2,1)S(1)}, bf16[2,128,256]{2,1,0:T(8,128)(2,1)S(1)}, u32[]{:S(2)}, u32[]{:S(2)}) %collective-permute-start.8) | collective-permute-done | bytes 131104 | tf_op jit(solution)/shard_map/ppermute | solution.py:323
  28.9 5.6 %collective-permute-done.9.refs_2_ = bf16[2,128,256]{2,1,0:T(8,128)(2,1)S(1)} collective-permute-done((bf16[2,128,256]{2,1,0:T(8,128)(2,1)S(1)}, bf16[2,128,256]{2,1,0:T(8,128)(2,1)S(1)}, u32[]{:S(2)}, u32[]{:S(2)}) %collective-permute-start.9) | collective-permute-done | bytes 131104 | tf_op jit(solution)/shard_map/ppermute | solution.py:323
  35.2 3.5 %collective-permute-done.2 = bf16[2,16,1024]{2,1,0:T(8,128)(2,1)S(1)} collective-permute-done((bf16[2,16,1024]{2,1,0:T(8,128)(2,1)S(1)}, bf16[2,16,1024]{2,1,0:T(8,128)(2,1)S(1)}, u32[]{:S(2)}, u32[]{:S(2)}) %collective-permute-start.2) | collective-permute-done | bytes 65568 | tf_op jit(solution)/shard_map/ppermute | solution.py:323
  38.7 1.7 %collective-permute-start.6 = (bf16[2,16,1024]{2,1,0:T(8,128)(2,1)S(1)}, bf16[2,16,1024]{2,1,0:T(8,128)(2,1)S(1)}, u32[]{:S(2)}, u32[]{:S(2)}) collective-permute-start(bf16[2,16,1024]{2,1,0:T(8,128)(2,1)S(1)} %pad_maximum_fusion.refs_4_), channel_id=1, source_target_pairs={{0,12},{1,13},{2,14},{3,15},{4,8},{5,9},{6,10},{7,11},{8,4},{9,5},... | collective-permute-start | bytes 196616 | tf_op jit(solution)/shard_map/ppermute | solution.py:323
  41.0 3.7 %collective-permute-done.3 = bf16[2,16,1024]{2,1,0:T(8,128)(2,1)S(1)} collective-permute-done((bf16[2,16,1024]{2,1,0:T(8,128)(2,1)S(1)}, bf16[2,16,1024]{2,1,0:T(8,128)(2,1)S(1)}, u32[]{:S(2)}, u32[]{:S(2)}) %collective-permute-start.3) | collective-permute-done | bytes 65568 | tf_op jit(solution)/shard_map/ppermute | solution.py:323
  46.4 3.5 %collective-permute-done.4 = bf16[2,16,1024]{2,1,0:T(8,128)(2,1)S(1)} collective-permute-done((bf16[2,16,1024]{2,1,0:T(8,128)(2,1)S(1)}, bf16[2,16,1024]{2,1,0:T(8,128)(2,1)S(1)}, u32[]{:S(2)}, u32[]{:S(2)}) %collective-permute-start.4) | collective-permute-done | bytes 65568 | tf_op jit(solution)/shard_map/ppermute | solution.py:323
  51.1 3.0 %collective-permute-done.5 = bf16[2,16,1024]{2,1,0:T(8,128)(2,1)S(1)} collective-permute-done((bf16[2,16,1024]{2,1,0:T(8,128)(2,1)S(1)}, bf16[2,16,1024]{2,1,0:T(8,128)(2,1)S(1)}, u32[]{:S(2)}, u32[]{:S(2)}) %collective-permute-start.5) | collective-permute-done | bytes 65568 | tf_op jit(solution)/shard_map/ppermute | solution.py:323
  55.4 3.0 %collective-permute-done.7 = bf16[2,16,1024]{2,1,0:T(8,128)(2,1)S(1)} collective-permute-done((bf16[2,16,1024]{2,1,0:T(8,128)(2,1)S(1)}, bf16[2,16,1024]{2,1,0:T(8,128)(2,1)S(1)}, u32[]{:S(2)}, u32[]{:S(2)}) %collective-permute-start.7) | collective-permute-done | bytes 65568 | tf_op jit(solution)/shard_map/ppermute | solution.py:323
  60.8 2.8 %collective-permute-start.19 = (bf16[128,256]{1,0:T(8,128)(2,1)S(1)}, bf16[128,256]{1,0:T(8,128)(2,1)S(1)}, u32[]{:S(2)}, u32[]{:S(2)}) collective-permute-start(bf16[128,256]{1,0:T(8,128)(2,1)S(1)} %shard_map.144), channel_id=1, source_target_pairs={{0,12},{1,13},{2,14},{3,15},{4,8},{5,9},{6,10},{7,11},{8,4},{9,5},... | collective-permute-start | bytes 196616 | tf_op jit(solution)/shard_map/ppermute | solution.py:323
  64.1 3.8 %collective-permute-done.14 = bf16[128,256]{1,0:T(8,128)(2,1)S(1)} collective-permute-done((bf16[128,256]{1,0:T(8,128)(2,1)S(1)}, bf16[128,256]{1,0:T(8,128)(2,1)S(1)}, u32[]{:S(2)}, u32[]{:S(2)}) %collective-permute-start.14) | collective-permute-done | bytes 65568 | tf_op jit(solution)/shard_map/ppermute | solution.py:323
  67.9 1.7 %collective-permute-start.17 = (bf16[128,256]{1,0:T(8,128)(2,1)S(1)}, bf16[128,256]{1,0:T(8,128)(2,1)S(1)}, u32[]{:S(2)}, u32[]{:S(2)}) collective-permute-start(bf16[128,256]{1,0:T(8,128)(2,1)S(1)} %shard_map.144), channel_id=1, source_target_pairs={{0,8},{1,9},{2,10},{3,11},{4,12},{5,13},{6,14},{7,15},{8,0},{9,1},... | collective-permute-start | bytes 196616 | tf_op jit(solution)/shard_map/ppermute | solution.py:323
  69.6 2.5 %collective-permute-done.15 = bf16[128,256]{1,0:T(8,128)(2,1)S(1)} collective-permute-done((bf16[128,256]{1,0:T(8,128)(2,1)S(1)}, bf16[128,256]{1,0:T(8,128)(2,1)S(1)}, u32[]{:S(2)}, u32[]{:S(2)}) %collective-permute-start.15) | collective-permute-done | bytes 65568 | tf_op jit(solution)/shard_map/ppermute | solution.py:323
  74.2 2.7 %collective-permute-done.16 = bf16[128,256]{1,0:T(8,128)(2,1)S(1)} collective-permute-done((bf16[128,256]{1,0:T(8,128)(2,1)S(1)}, bf16[128,256]{1,0:T(8,128)(2,1)S(1)}, u32[]{:S(2)}, u32[]{:S(2)}) %collective-permute-start.16) | collective-permute-done | bytes 65568 | tf_op jit(solution)/shard_map/ppermute | solution.py:323
  77.5 3.7 %collective-permute-done.18 = bf16[128,256]{1,0:T(8,128)(2,1)S(1)} collective-permute-done((bf16[128,256]{1,0:T(8,128)(2,1)S(1)}, bf16[128,256]{1,0:T(8,128)(2,1)S(1)}, u32[]{:S(2)}, u32[]{:S(2)}) %collective-permute-start.18) | collective-permute-done | bytes 65568 | tf_op jit(solution)/shard_map/ppermute | solution.py:323
  81.3 1.6 %copy-done.2 = bf16[2,384,2048]{2,1,0:T(8,128)(2,1)} copy-done((bf16[2,384,2048]{2,1,0:T(8,128)(2,1)}, bf16[2,384,2048]{2,1,0:T(8,128)(2,1)S(1)}, u32[]{:S(2)}) %copy-start.2) | copy-done | bytes 3145752
  82.9 6.9 %shard_map.145 = (bf16[16,2048]{1,0:T(8,128)(2,1)}, bf16[2,16,2048]{2,1,0:T(8,128)(2,1)S(1)}, bf16[2,16,2048]{2,1,0:T(8,128)(2,1)S(1)}, bf16[2,16,2048]{2,1,0:T(8,128)(2,1)S(1)}, bf16[2,16,2048]{2,1,0:T(8,128)(2,1)S(1)}) custom-call(s32[1]{0:T(128)} %bitcast.at_ref, bf16[8,128,256]{2,1,0:T(8,128)(2,1)S(1)} %bitcast_dynamic-update-slice_fusion.rows_ref, ...), custom_call_target="tpu_custom_call" | custom-call | flops 2415919104 | bytes 18874368 | tf_op jit(solution)/shard_map/pallas_call | solution.py:30
  90.4 1.5 %collective-permute-start.27 = (bf16[2,16,2048]{2,1,0:T(8,128)(2,1)S(1)}, bf16[2,16,2048]{2,1,0:T(8,128)(2,1)S(1)}, u32[]{:S(2)}, u32[]{:S(2)}) collective-permute-start(bf16[2,16,2048]{2,1,0:T(8,128)(2,1)S(1)} %get-tuple-element.33), channel_id=1, source_target_pairs={{0,2},{1,3},{2,0},{3,1},{4,6},{5,7},{6,4},{7,5},{8,10},{9,11},{10,... | collective-permute-start | bytes 393224 | tf_op jit(solution)/shard_map/ppermute | solution.py:323
  91.9 2.9 %collective-permute-done.24.piece_ref = bf16[2,16,2048]{2,1,0:T(8,128)(2,1)S(1)} collective-permute-done((bf16[2,16,2048]{2,1,0:T(8,128)(2,1)S(1)}, bf16[2,16,2048]{2,1,0:T(8,128)(2,1)S(1)}, u32[]{:S(2)}, u32[]{:S(2)}) %collective-permute-start.24) | collective-permute-done | bytes 131104 | tf_op jit(solution)/shard_map/ppermute | solution.py:323
  96.6 2.9 %collective-permute-start.28 = (bf16[16,2048]{1,0:T(8,128)(2,1)S(1)}, bf16[16,2048]{1,0:T(8,128)(2,1)S(1)}, u32[]{:S(2)}, u32[]{:S(2)}) collective-permute-start(bf16[16,2048]{1,0:T(8,128)(2,1)S(1)} %get-tuple-element.34), channel_id=1, source_target_pairs={{0,4},{1,5},{2,6},{3,7},{4,0},{5,1},{6,2},{7,3},{8,12},{9,13},{10,... | collective-permute-start | bytes 196616 | tf_op jit(solution)/shard_map/ppermute | solution.py:323
  99.4 1.6 %collective-permute-done.25 = bf16[16,2048]{1,0:T(8,128)(2,1)S(1)} collective-permute-done((bf16[16,2048]{1,0:T(8,128)(2,1)S(1)}, bf16[16,2048]{1,0:T(8,128)(2,1)S(1)}, u32[]{:S(2)}, u32[]{:S(2)}) %collective-permute-start.25) | collective-permute-done | bytes 65568 | tf_op jit(solution)/shard_map/ppermute | solution.py:323
  (73 shorter events, 22.0 us)
Async XLA Ops:
  2.4 14.9 %all-to-all-start = ((bf16[2,16,1664]{2,0,1:T(2,128)(2,1)}), bf16[2,16,1664]{2,0,1:T(2,128)(2,1)S(1)}, u32[]{:S(2)}, u32[]{:S(2)}) async-start(bf16[2,16,1664]{2,0,1:T(2,128)(2,1)} %copy.17), calls=%async_computation | async-start | bytes 212992 | tf_op jit(solution)/shard_map/all_to_all | solution.py:386
  20.1 6.4 %collective-permute-start = (bf16[16,1024]{1,0:T(8,128)(2,1)S(1)}, bf16[16,1024]{1,0:T(8,128)(2,1)S(1)}, u32[]{:S(2)}, u32[]{:S(2)}) collective-permute-start(bf16[16,1024]{1,0:T(8,128)(2,1)S(1)} %get-tuple-element.20), channel_id=1, source_target_pairs={{0,1},{1,0},{2,3},{3,2},{4,5},{5,4},{6,7},{7,6},{8,9},{9,8},{10,11... | collective-permute-start | bytes 98312 | tf_op jit(solution)/shard_map/ppermute | solution.py:323
  21.3 7.5 %collective-permute-start.8 = (bf16[2,128,256]{2,1,0:T(8,128)(2,1)S(1)}, bf16[2,128,256]{2,1,0:T(8,128)(2,1)S(1)}, u32[]{:S(2)}, u32[]{:S(2)}) collective-permute-start(bf16[2,128,256]{2,1,0:T(8,128)(2,1)S(1)} %get-tuple-element.22), channel_id=1, source_target_pairs={{0,4},{1,5},{2,6},{3,7},{4,0},{5,1},{6,2},{7,3},{8,12},{9,13},{10,... | collective-permute-start | bytes 393224 | tf_op jit(solution)/shard_map/ppermute | solution.py:323
  21.5 12.9 %collective-permute-start.9 = (bf16[2,128,256]{2,1,0:T(8,128)(2,1)S(1)}, bf16[2,128,256]{2,1,0:T(8,128)(2,1)S(1)}, u32[]{:S(2)}, u32[]{:S(2)}) collective-permute-start(bf16[2,128,256]{2,1,0:T(8,128)(2,1)S(1)} %get-tuple-element.23), channel_id=1, source_target_pairs={{0,8},{1,9},{2,10},{3,11},{4,12},{5,13},{6,14},{7,15},{8,0},{9,1},... | collective-permute-start | bytes 393224 | tf_op jit(solution)/shard_map/ppermute | solution.py:323
  22.8 11.7 %collective-permute-start.10 = (bf16[2,128,256]{2,1,0:T(8,128)(2,1)S(1)}, bf16[2,128,256]{2,1,0:T(8,128)(2,1)S(1)}, u32[]{:S(2)}, u32[]{:S(2)}) collective-permute-start(bf16[2,128,256]{2,1,0:T(8,128)(2,1)S(1)} %get-tuple-element.24), channel_id=1, source_target_pairs={{0,12},{1,13},{2,14},{3,15},{4,8},{5,9},{6,10},{7,11},{8,4},{9,5},... | collective-permute-start | bytes 393224 | tf_op jit(solution)/shard_map/ppermute | solution.py:323
  25.8 55.5 %collective-permute-start.21 = (bf16[2,2048,384]{2,1,0:T(8,128)(2,1)}, bf16[2,2048,384]{2,1,0:T(8,128)(2,1)S(1)}, u32[]{:S(2)}, u32[]{:S(2)}) collective-permute-start(bf16[2,2048,384]{2,1,0:T(8,128)(2,1)} %gate_ref.1), channel_id=1, source_target_pairs={{0,1},{1,0},{2,3},{3,2},{4,5},{5,4},{6,7},{7,6},{8,9},{9,8},{10,11... | collective-permute-start | bytes 9437192 | tf_op jit(solution)/shard_map/ppermute | solution.py:323
  26.5 54.8 %collective-permute-start.22 = (bf16[2,2048,384]{2,1,0:T(8,128)(2,1)}, bf16[2,2048,384]{2,1,0:T(8,128)(2,1)S(1)}, u32[]{:S(2)}, u32[]{:S(2)}) collective-permute-start(bf16[2,2048,384]{2,1,0:T(8,128)(2,1)} %up_ref.1), channel_id=1, source_target_pairs={{0,1},{1,0},{2,3},{3,2},{4,5},{5,4},{6,7},{7,6},{8,9},{9,8},{10,11... | collective-permute-start | bytes 9437192 | tf_op jit(solution)/shard_map/ppermute | solution.py:323
  28.9 52.5 %collective-permute-start.23 = (bf16[2,384,2048]{2,1,0:T(8,128)(2,1)}, bf16[2,384,2048]{2,1,0:T(8,128)(2,1)S(1)}, u32[]{:S(2)}, u32[]{:S(2)}) collective-permute-start(bf16[2,384,2048]{2,1,0:T(8,128)(2,1)} %down_hbm.1), channel_id=1, source_target_pairs={{0,1},{1,0},{2,3},{3,2},{4,5},{5,4},{6,7},{7,6},{8,9},{9,8},{10,11... | collective-permute-start | bytes 9437192 | tf_op jit(solution)/shard_map/ppermute | solution.py:323
  34.4 6.0 %collective-permute-start.1 = (bf16[2,16,1024]{2,1,0:T(8,128)(2,1)S(1)}, bf16[2,16,1024]{2,1,0:T(8,128)(2,1)S(1)}, u32[]{:S(2)}, u32[]{:S(2)}) collective-permute-start(bf16[2,16,1024]{2,1,0:T(8,128)(2,1)S(1)} %pad_maximum_fusion.refs_4_), channel_id=1, source_target_pairs={{0,2},{1,3},{2,0},{3,1},{4,6},{5,7},{6,4},{7,5},{8,10},{9,11},{10,... | collective-permute-start | bytes 196616 | tf_op jit(solution)/shard_map/ppermute | solution.py:323
  38.7 7.1 %collective-permute-start.6 = (bf16[2,16,1024]{2,1,0:T(8,128)(2,1)S(1)}, bf16[2,16,1024]{2,1,0:T(8,128)(2,1)S(1)}, u32[]{:S(2)}, u32[]{:S(2)}) collective-permute-start(bf16[2,16,1024]{2,1,0:T(8,128)(2,1)S(1)} %pad_maximum_fusion.refs_4_), channel_id=1, source_target_pairs={{0,12},{1,13},{2,14},{3,15},{4,8},{5,9},{6,10},{7,11},{8,4},{9,5},... | collective-permute-start | bytes 196616 | tf_op jit(solution)/shard_map/ppermute | solution.py:323
  40.4 4.3 %collective-permute-start.3 = (bf16[2,16,1024]{2,1,0:T(8,128)(2,1)S(1)}, bf16[2,16,1024]{2,1,0:T(8,128)(2,1)S(1)}, u32[]{:S(2)}, u32[]{:S(2)}) collective-permute-start(bf16[2,16,1024]{2,1,0:T(8,128)(2,1)S(1)} %collective-permute-done.2), channel_id=1, source_target_pairs={{0,2},{1,3},{2,0},{3,1},{4,6},{5,7},{6,4},{7,5},{8,10},{9,11},{10,... | collective-permute-start | bytes 196616 | tf_op jit(solution)/shard_map/ppermute | solution.py:323
  44.7 5.2 %collective-permute-start.4 = (bf16[2,16,1024]{2,1,0:T(8,128)(2,1)S(1)}, bf16[2,16,1024]{2,1,0:T(8,128)(2,1)S(1)}, u32[]{:S(2)}, u32[]{:S(2)}) collective-permute-start(bf16[2,16,1024]{2,1,0:T(8,128)(2,1)S(1)} %pad_maximum_fusion.refs_4_), channel_id=1, source_target_pairs={{0,8},{1,9},{2,10},{3,11},{4,12},{5,13},{6,14},{7,15},{8,0},{9,1},... | collective-permute-start | bytes 196616 | tf_op jit(solution)/shard_map/ppermute | solution.py:323
  45.8 12.6 %collective-permute-start.12 = (bf16[4,128,256]{2,1,0:T(8,128)(2,1)S(1)}, bf16[4,128,256]{2,1,0:T(8,128)(2,1)S(1)}, u32[]{:S(2)}, u32[]{:S(2)}) collective-permute-start(bf16[4,128,256]{2,1,0:T(8,128)(2,1)S(1)} %get-tuple-element.26), channel_id=1, source_target_pairs={{0,2},{1,3},{2,0},{3,1},{4,6},{5,7},{6,4},{7,5},{8,10},{9,11},{10,... | collective-permute-start | bytes 786440 | tf_op jit(solution)/shard_map/ppermute | solution.py:323
  49.8 4.3 %collective-permute-start.5 = (bf16[2,16,1024]{2,1,0:T(8,128)(2,1)S(1)}, bf16[2,16,1024]{2,1,0:T(8,128)(2,1)S(1)}, u32[]{:S(2)}, u32[]{:S(2)}) collective-permute-start(bf16[2,16,1024]{2,1,0:T(8,128)(2,1)S(1)} %collective-permute-done.4), channel_id=1, source_target_pairs={{0,2},{1,3},{2,0},{3,1},{4,6},{5,7},{6,4},{7,5},{8,10},{9,11},{10,... | collective-permute-start | bytes 196616 | tf_op jit(solution)/shard_map/ppermute | solution.py:323
  60.8 7.1 %collective-permute-start.19 = (bf16[128,256]{1,0:T(8,128)(2,1)S(1)}, bf16[128,256]{1,0:T(8,128)(2,1)S(1)}, u32[]{:S(2)}, u32[]{:S(2)}) collective-permute-start(bf16[128,256]{1,0:T(8,128)(2,1)S(1)} %shard_map.144), channel_id=1, source_target_pairs={{0,12},{1,13},{2,14},{3,15},{4,8},{5,9},{6,10},{7,11},{8,4},{9,5},... | collective-permute-start | bytes 196616 | tf_op jit(solution)/shard_map/ppermute | solution.py:323
  63.6 4.3 %collective-permute-start.14 = (bf16[128,256]{1,0:T(8,128)(2,1)S(1)}, bf16[128,256]{1,0:T(8,128)(2,1)S(1)}, u32[]{:S(2)}, u32[]{:S(2)}) collective-permute-start(bf16[128,256]{1,0:T(8,128)(2,1)S(1)} %shard_map.144), channel_id=1, source_target_pairs={{0,2},{1,3},{2,0},{3,1},{4,6},{5,7},{6,4},{7,5},{8,10},{9,11},{10,... | collective-permute-start | bytes 196616 | tf_op jit(solution)/shard_map/ppermute | solution.py:323
  67.9 5.2 %collective-permute-start.17 = (bf16[128,256]{1,0:T(8,128)(2,1)S(1)}, bf16[128,256]{1,0:T(8,128)(2,1)S(1)}, u32[]{:S(2)}, u32[]{:S(2)}) collective-permute-start(bf16[128,256]{1,0:T(8,128)(2,1)S(1)} %shard_map.144), channel_id=1, source_target_pairs={{0,8},{1,9},{2,10},{3,11},{4,12},{5,13},{6,14},{7,15},{8,0},{9,1},... | collective-permute-start | bytes 196616 | tf_op jit(solution)/shard_map/ppermute | solution.py:323
  72.1 4.8 %collective-permute-start.16 = (bf16[128,256]{1,0:T(8,128)(2,1)S(1)}, bf16[128,256]{1,0:T(8,128)(2,1)S(1)}, u32[]{:S(2)}, u32[]{:S(2)}) collective-permute-start(bf16[128,256]{1,0:T(8,128)(2,1)S(1)} %collective-permute-done.15), channel_id=1, source_target_pairs={{0,2},{1,3},{2,0},{3,1},{4,6},{5,7},{6,4},{7,5},{8,10},{9,11},{10,... | collective-permute-start | bytes 196616 | tf_op jit(solution)/shard_map/ppermute | solution.py:323
  73.1 8.1 %collective-permute-start.20 = (bf16[128,256]{1,0:T(8,128)(2,1)S(1)}, bf16[128,256]{1,0:T(8,128)(2,1)S(1)}, u32[]{:S(2)}, u32[]{:S(2)}) collective-permute-start(bf16[128,256]{1,0:T(8,128)(2,1)S(1)} %collective-permute-done.19), channel_id=1, source_target_pairs={{0,2},{1,3},{2,0},{3,1},{4,6},{5,7},{6,4},{7,5},{8,10},{9,11},{10,... | collective-permute-start | bytes 196616 | tf_op jit(solution)/shard_map/ppermute | solution.py:323
  89.8 5.0 %collective-permute-start.24 = (bf16[2,16,2048]{2,1,0:T(8,128)(2,1)S(1)}, bf16[2,16,2048]{2,1,0:T(8,128)(2,1)S(1)}, u32[]{:S(2)}, u32[]{:S(2)}) collective-permute-start(bf16[2,16,2048]{2,1,0:T(8,128)(2,1)S(1)} %get-tuple-element.29), channel_id=1, source_target_pairs={{0,2},{1,3},{2,0},{3,1},{4,6},{5,7},{6,4},{7,5},{8,10},{9,11},{10,... | collective-permute-start | bytes 393224 | tf_op jit(solution)/shard_map/ppermute | solution.py:323
  90.4 6.1 %collective-permute-start.27 = (bf16[2,16,2048]{2,1,0:T(8,128)(2,1)S(1)}, bf16[2,16,2048]{2,1,0:T(8,128)(2,1)S(1)}, u32[]{:S(2)}, u32[]{:S(2)}) collective-permute-start(bf16[2,16,2048]{2,1,0:T(8,128)(2,1)S(1)} %get-tuple-element.33), channel_id=1, source_target_pairs={{0,2},{1,3},{2,0},{3,1},{4,6},{5,7},{6,4},{7,5},{8,10},{9,11},{10,... | collective-permute-start | bytes 393224 | tf_op jit(solution)/shard_map/ppermute | solution.py:323
  94.9 6.2 %collective-permute-start.25 = (bf16[16,2048]{1,0:T(8,128)(2,1)S(1)}, bf16[16,2048]{1,0:T(8,128)(2,1)S(1)}, u32[]{:S(2)}, u32[]{:S(2)}) collective-permute-start(bf16[16,2048]{1,0:T(8,128)(2,1)S(1)} %get-tuple-element.30), channel_id=1, source_target_pairs={{0,12},{1,13},{2,14},{3,15},{4,8},{5,9},{6,10},{7,11},{8,4},{9,5},... | collective-permute-start | bytes 196616 | tf_op jit(solution)/shard_map/ppermute | solution.py:323
  96.1 6.3 %collective-permute-start.26 = (bf16[16,2048]{1,0:T(8,128)(2,1)S(1)}, bf16[16,2048]{1,0:T(8,128)(2,1)S(1)}, u32[]{:S(2)}, u32[]{:S(2)}) collective-permute-start(bf16[16,2048]{1,0:T(8,128)(2,1)S(1)} %get-tuple-element.31), channel_id=1, source_target_pairs={{0,8},{1,9},{2,10},{3,11},{4,12},{5,13},{6,14},{7,15},{8,0},{9,1},... | collective-permute-start | bytes 196616 | tf_op jit(solution)/shard_map/ppermute | solution.py:323
  96.6 5.8 %collective-permute-start.28 = (bf16[16,2048]{1,0:T(8,128)(2,1)S(1)}, bf16[16,2048]{1,0:T(8,128)(2,1)S(1)}, u32[]{:S(2)}, u32[]{:S(2)}) collective-permute-start(bf16[16,2048]{1,0:T(8,128)(2,1)S(1)} %get-tuple-element.34), channel_id=1, source_target_pairs={{0,4},{1,5},{2,6},{3,7},{4,0},{5,1},{6,2},{7,3},{8,12},{9,13},{10,... | collective-permute-start | bytes 196616 | tf_op jit(solution)/shard_map/ppermute | solution.py:323
  (9 other events, 153.3 us)
where the time goes:
time: 103 us
  waiting for transfers between devices  51.3 us (50%)
  starting transfers between devices  34 us (33%)
  Pallas kernels  12.4 us (12%)
  local copies, waits for them, and re-layouts  3.93 us (4%)
    ppermute x29, waiting for transfers between devices, swap(): return lax.ppermute(value, 'seq', [(i, i ^ offset) for i in range(count)])  44.5 us
    ppermute x29, starting transfers between devices, swap(): return lax.ppermute(value, 'seq', [(i, i ^ offset) for i in range(count)])  26.5 us
    pallas_call x8, Pallas kernels, call(): pl.pallas_call(kernel, out_shape=tuple((jax.ShapeDtypeStruct(s, d) for s,...  12.4 us
    all_to_all x1, starting transfers between devices, exchange_body(): taken = lax.all_to_all(sent, 'seq', split_axis=1, concat_axis=0, tiled=True)  7.41 us
    all_to_all x1, waiting for transfers between devices, exchange_body(): taken = lax.all_to_all(sent, 'seq', split_axis=1, concat_axis=0, tiled=True)  6.74 us
    unnamed x20, local copies, waits for them, and re-layouts  2.46 us
  transfers between devices with their start and end apart: 30, of which 18 were waited for; matrix products, arithmetic and copies ran while one was open for 2% of the time, Pallas kernels for 2%

commit v1 on v0

--- a/solution.py
+++ b/solution.py
@@ -94,13 +94,16 @@
 
 
 def split_kernel(at_ref, weight_hbm, *refs):
-    parts, weight_ref, sems = refs[:-2], *refs[-2:]
-    fetch((weight_hbm,), (weight_ref,), sems)[0].wait()
+    parts, sems = refs[:-1], refs[-1]
     chip = at_ref[0] // 2
-    for k, part in enumerate(parts):
+    sources, targets = [], []
+    for k, part in reversed(list(enumerate(parts))):
         for y in range(2):
             start = pl.multiple_of((chip ^ (2 * k + y)) * part.shape[2], LANES)
-            part[y] = weight_ref[:, pl.ds(start, part.shape[2])]
+            sources.append(weight_hbm.at[:, pl.ds(start, part.shape[2])])
+            targets.append(part.at[y])
+    for copy in fetch(sources, targets, sems):
+        copy.wait()
 
 
 def regroup_kernel(*refs):
@@ -195,10 +198,11 @@
     send_ref[...] = result[half:]
 
 
-def project_kernel(at_ref, rows_ref, *refs):
-    columns, (out_ref, weight_ref) = refs[:-2], refs[-2:]
+def project_kernel(at_ref, *refs):
+    pieces, columns, (out_ref, weight_ref) = refs[:-6], refs[-6:-2], refs[-2:]
     me = at_ref[0]
-    members, _, places, wide = rows_ref.shape
+    members = len(pieces)
+    _, places, wide = pieces[0].shape
     rows = members * places
     owned = columns[0].shape[1]
     for i, ref in enumerate(columns):
@@ -209,7 +213,7 @@
     for half in range(KVH):
         start = pl.multiple_of((me ^ half) % KVH * wide, wide)
         total = total + jnp.dot(
-            rows_ref[:, half].reshape(rows, wide),
+            jnp.concatenate([piece[half] for piece in pieces], axis=0),
             weight_ref[pl.ds(start, wide), :],
             preferred_element_type=jnp.float32,
         )
@@ -221,26 +225,75 @@
     ).astype(jnp.bfloat16)
 
 
+def weigh(chip, odd, pieces, gain_ref, there, own_hbm, own_ref, sems):
+    lanes = pieces[0].shape[1]
+    experts = own_ref.shape[2]
+    starts = [
+        pl.multiple_of((chip ^ (2 * i + odd)) * lanes, lanes) for i in range(len(pieces))
+    ]
+    sources, targets = [], []
+    for i, start in enumerate(starts):
+        for m, source in enumerate(own_hbm):
+            sources.append(source.at[:, pl.ds(start, lanes), :])
+            targets.append(own_ref.at[m, i])
+    copies = fetch(sources, targets, sems)
+    rows = [
+        (
+            piece[...].astype(jnp.float32) * gain_ref[:, pl.ds(start, lanes)].astype(jnp.float32)
+        ).astype(jnp.bfloat16)
+        for piece, start in zip(pieces, starts)
+    ]
+
+    def products(pick):
+        return [
+            sum(
+                jnp.dot(row, pick(m, i, e), preferred_element_type=jnp.float32)
+                for i, row in enumerate(rows)
+            )
+            for e in range(experts)
+            for m in range(2)
+        ]
+
+    out = products(lambda m, i, e: there[m][e, pl.ds(starts[i], lanes), :])
+    for copy in copies:
+        copy.wait()
+    return out + products(lambda m, i, e: own_ref[m, i, e])
+
+
+def gate_kernel(at_ref, gain_ref, gate_ref, up_ref, gate_hbm, up_hbm, *refs):
+    pieces, (out_ref, own_ref, sems) = refs[:-3], refs[-3:]
+    out = weigh(
+        at_ref[0] // 2, 0, pieces, gain_ref, (gate_ref, up_ref), (gate_hbm, up_hbm), own_ref, sems
+    )
+    for i, value in enumerate(out):
+        out_ref[i] = value
+
+
+def block_order(chips):
+    near = range(chips - 2, -1, -2)
+    return [k + 1 for k in near] + list(near)
+
+
 def expert_kernel(
     per_rows,
+    chips,
     at_ref,
-    rows_ref,
     gain_ref,
-    info_ref,
     gate_ref,
     up_ref,
-    gate_peer_ref,
-    up_peer_ref,
+    gate_hbm,
+    up_hbm,
+    partial_ref,
+    info_ref,
+    down_ref,
     down_hbm,
-    down_peer_hbm,
-    projected_ref,
     *refs,
 ):
-    outs, (normed_ref, down_ref, down_peer_ref, sems) = refs[:-4], refs[-4:]
-    copies = fetch((down_hbm, down_peer_hbm), (down_ref, down_peer_ref), sems)
+    near, far, projected_ref = refs[: chips // 2], refs[chips // 2 : chips], refs[chips]
+    outs, (result_ref, own_ref, down_own_ref, sems, down_sems) = refs[chips + 1 : -5], refs[-5:]
     me = at_ref[0]
     chip, core = me // 2, me % 2
-    chips, rows, lanes = rows_ref.shape
+    rows, lanes = near[0].shape
     new = info_ref.shape[0]
     per_dev = rows // chips
     members = per_dev // per_rows
@@ -248,67 +301,50 @@
     width = info_ref.shape[1] // 3
 
     squares = jnp.zeros((rows, lanes), jnp.float32)
-    for i in range(chips):
-        piece = rows_ref[i].astype(jnp.float32)
-        squares = squares + piece * piece
-    inverse = lax.rsqrt(jnp.sum(squares, axis=1, keepdims=True) / (chips * lanes) + 1e-06)
     own = pl.ds(pl.multiple_of(chip * per_dev, per_dev), per_dev)
     for i in range(chips):
-        at = pl.ds(pl.multiple_of((chip ^ i) * lanes, lanes), lanes)
-        gain = gain_ref[:, at].astype(jnp.float32)
-        normed_ref[:, at] = (rows_ref[i].astype(jnp.float32) * inverse * gain).astype(jnp.bfloat16)
-        projected_ref[:, at] = rows_ref[i, own, :]
-    normed = jnp.concatenate(
-        [
-            normed_ref[pl.ds(pl.multiple_of((chip ^ i) * per_dev, per_dev), per_dev), :]
-            for i in range(chips)
-        ],
-        axis=0,
-    )
-
-    def token(shape):
-        r = iota(shape, 0)
-        return ((r // per_dev) ^ chip) * per_dev + r % per_dev
-
-    place = token((rows, new)) // members
-    spread = iota((rows, new), 1) == position_of(place, per_rows, core)
+        ref = (far if i % 2 else near)[i // 2]
+        piece = ref[...].astype(jnp.float32)
+        squares = squares + piece * piece
+        projected_ref[:, pl.ds(pl.multiple_of((chip ^ i) * lanes, lanes), lanes)] = ref[own, :]
+    inverse = lax.rsqrt(jnp.sum(squares, axis=1, keepdims=True) / (chips * lanes) + 1e-06)
+
+    token = iota((rows, new), 0)
+    spread = iota((rows, new), 1) == position_of(token // members, per_rows, core)
     info = jnp.dot(
         spread.astype(jnp.bfloat16), info_ref[...], preferred_element_type=jnp.float32
     )
-    mine = iota((rows, width), 1) // TOPK == token((rows, width)) % members
+    mine = iota((rows, width), 1) // TOPK == iota((rows, width), 0) % members
     share = jnp.where(mine, info[:, width : 2 * width] + info[:, 2 * width :], 0.0)
     whole = jnp.sum(share, axis=1, keepdims=True)
+
+    (copy,) = fetch((down_hbm,), (down_own_ref,), down_sems)
+    out = weigh(
+        chip, 1, far, gain_ref, (gate_ref, up_ref), (gate_hbm, up_hbm), own_ref, sems
+    )
     hidden = []
-    for device, gates, ups in ((me, gate_ref, up_ref), (me ^ 1, gate_peer_ref, up_peer_ref)):
-        for e in range(experts):
-            chosen = info[:, :width] == (device * experts + e).astype(jnp.float32)
-            scale = jnp.sum(jnp.where(chosen, share, 0.0), axis=1, keepdims=True) / whole
-            gate = jnp.dot(normed, gates[e], preferred_element_type=jnp.float32)
-            up = jnp.dot(normed, ups[e], preferred_element_type=jnp.float32)
-            hidden.append((gate / (1.0 + jnp.exp(-gate)) * up * scale).astype(jnp.bfloat16))
-    for copy in copies:
-        copy.wait()
-    order = block_order(chips)
+    for d in range(2 * experts):
+        device = me ^ (1 - d // experts)
+        chosen = info[:, :width] == (device * experts + d % experts).astype(jnp.float32)
+        scale = jnp.sum(jnp.where(chosen, share, 0.0), axis=1, keepdims=True) / whole
+        gate = (partial_ref[2 * d] + out[2 * d]) * inverse
+        up = (partial_ref[2 * d + 1] + out[2 * d + 1]) * inverse
+        hidden.append((gate / (1.0 + jnp.exp(-gate)) * up * scale).astype(jnp.bfloat16))
+    copy.wait()
     step = 512
     for at in range(0, down_ref.shape[2], step):
         part = jnp.zeros((rows, step), jnp.float32)
-        for e, value in enumerate(hidden):
-            ref = (down_ref, down_peer_ref)[e // experts]
+        for d, value in enumerate(hidden):
+            ref = (down_ref, down_own_ref)[d // experts]
             part = part + jnp.dot(
-                value, ref[e % experts, :, at : at + step], preferred_element_type=jnp.float32
+                value, ref[d % experts, :, at : at + step], preferred_element_type=jnp.float32
             )
-        part = part.astype(jnp.bfloat16)
-        block = 0
-        for out in outs:
-            for i in range(out.shape[0]):
-                where = order[block]
-                out[i, :, at : at + step] = part[where * per_dev : (where + 1) * per_dev]
-                block += 1
-
-
-def block_order(chips):
-    near = range(chips - 2, -1, -2)
-    return [k + 1 for k in near] + list(near)
+        result_ref[:, at : at + step] = part.astype(jnp.bfloat16)
+    order = iter(block_order(chips))
+    for out in outs:
+        for i in range(out.shape[0]):
+            start = pl.multiple_of((chip ^ next(order)) * per_dev, per_dev)
+            out[i] = result_ref[pl.ds(start, per_dev), :]
 
 
 def add_kernel(near_ref, piece_ref, *outs):
@@ -342,10 +378,6 @@
     near = [own] + [swap(own, k) for k in range(count - 4, 0, -4)][::-1]
     far = [swap(piece, 2) for piece in near]
     return near, far
-
-
-def interleave(near, far):
-    return jnp.stack([p for pair in zip(near, far) for p in pair], axis=0)
 
 
 def exchange_body(
@@ -394,7 +426,7 @@
         split_kernel,
         [((2, owned, lanes), bf16)] * (chips // 2),
         (at, out_weight),
-        scratch=[pltpu.VMEM(out_weight.shape, bf16), pltpu.SemaphoreType.DMA((1,))],
+        scratch=[pltpu.SemaphoreType.DMA((chips,))],
         far=(1,),
         moved=4 * out_weight.size,
     )
@@ -416,50 +448,67 @@
     )
     peer = swap(send, 1)
     own = jnp.stack([keep, peer])
-    heads = interleave(*gather_rows(own))
-    near, far = call(
+    near, far = gather_rows(own)
+    heads = [piece for pair in zip(near, far) for piece in pair]
+    columns, across = call(
         regroup_kernel,
         [((chips // 2, owned, lanes), bf16)] * 2,
         (*parts, own),
         loose=(len(parts),),
     )
-    beyond = swap(far, 2)
+    beyond = swap(across, 2)
+    beyond_peer = swap(beyond, 1)
     half = rows // 2
     (projected,) = call(
         project_kernel,
         [((half, lanes), bf16)],
-        (at, heads, near, swap(near, 1), beyond, swap(beyond, 1)),
+        (at, *heads, columns, swap(columns, 1), beyond, beyond_peer),
         scratch=[pltpu.VMEM((D, lanes), bf16)],
         flops=2 * half * D * lanes,
         moved=4 * half * D,
     )
-    gathered = interleave(*gather_rows(projected))
-    info = taken[:, wide + 2 * HD :]
+    near, far = gather_rows(projected)
+    gain = norm_gain.reshape(1, D)
+    experts, _, hidden = w_gate.shape
+    own_rows = pltpu.VMEM((2, chips // 2, experts, lanes, hidden), bf16)
+    (partial,) = call(
+        gate_kernel,
+        [((4 * experts, half, hidden), jnp.float32)],
+        (at, gain, gate_peer, up_peer, w_gate, w_up, *near),
+        scratch=[own_rows, pltpu.SemaphoreType.DMA((chips,))],
+        far=(4, 5),
+        vmem_mib=16,
+        flops=4 * half * w_gate.size,
+        moved=4 * w_gate.size,
+    )
     projected, *blocks = call(
-        functools.partial(expert_kernel, per_rows),
+        functools.partial(expert_kernel, per_rows, chips),
         [((per_dev, D), bf16)] + [((2, per_dev, D), bf16)] * (chips // 2),
         (
             at,
-            gathered,
-            norm_gain.reshape(1, D),
-            info,
+            gain,
+            gate_peer,
+            up_peer,
             w_gate,
             w_up,
-            gate_peer,
-            up_peer,
+            partial,
+            taken[:, wide + 2 * HD :],
+            down_peer,
             w_down,
-            down_peer,
+            *near,
+            *far,
         ),
         scratch=[
             pltpu.VMEM((half, D), bf16),
+            own_rows,
             pltpu.VMEM(w_down.shape, bf16),
-            pltpu.VMEM(w_down.shape, bf16),
-            pltpu.SemaphoreType.DMA((2,)),
+            pltpu.SemaphoreType.DMA((chips,)),
+            pltpu.SemaphoreType.DMA((1,)),
         ],
-        far=(8, 9),
-        vmem_mib=30,
-        flops=12 * half * w_gate.size,
-        moved=12 * w_gate.size,
+        far=(4, 5, 9),
+        vmem_mib=24,
+        flops=8 * half * w_gate.size,
+        moved=8 * w_gate.size,
     )
     pieces = scatter_pieces(blocks[: chips // 4], blocks[chips // 4 :])
     mixed = sum(piece.astype(jnp.float32) for piece in pieces)

time: 103 us -> 107 us (1.039)
  Pallas kernels: 12.4 us -> 18.9 us
  waiting for transfers between devices: 51.3 us -> 45.3 us
  starting transfers between devices: 34 us -> 36.4 us
    pallas_call x8 -> x9, Pallas kernels: 12.4 us -> 18.9 us  [call(): pl.pallas_call(kernel, out_shape=tuple((jax.ShapeDtypeStruct(s, d) for s,...]
    all_to_all x1, waiting for transfers between devices: 6.74 us -> 1.8 us  [exchange_body(): taken = lax.all_to_all(sent, 'seq', split_axis=1, concat_axis=0, tiled=True)]
    ppermute x29, starting transfers between devices: 26.5 us -> 29.4 us  [swap(): return lax.ppermute(value, 'seq', [(i, i ^ offset) for i in range(count)])]
    ppermute x29, waiting for transfers between devices: 44.5 us -> 43.5 us  [swap(): return lax.ppermute(value, 'seq', [(i, i ^ offset) for i in range(count)])]
    unnamed x20 -> x9, local copies, waits for them, and re-layouts: 2.46 us -> 2.71 us
  transfers between devices with their start and end apart: 30 -> 30, of which waited for: 18 -> 17; matrix products, arithmetic and copies ran while one was open for 2% -> 2% of each run, Pallas kernels for 2% -> 10%
where the time goes in v1:
time: 107 us; the launch traced here: 106 us
  waiting for transfers between devices  45.3 us (42%)
  starting transfers between devices  36.4 us (34%)
  Pallas kernels  18.9 us (18%)
  local copies, waits for them, and re-layouts  4.38 us (4%)
    ppermute x29, waiting for transfers between devices, swap(): return lax.ppermute(value, 'seq', [(i, i ^ offset) for i in range(count)])  43.5 us
    ppermute x29, starting transfers between devices, swap(): return lax.ppermute(value, 'seq', [(i, i ^ offset) for i in range(count)])  29.4 us
    pallas_call x9, Pallas kernels, call(): pl.pallas_call(kernel, out_shape=tuple((jax.ShapeDtypeStruct(s, d) for s,...  18.9 us
    all_to_all x1, starting transfers between devices, exchange_body(): taken = lax.all_to_all(sent, 'seq', split_axis=1, concat_axis=0, tiled=True)  7.04 us
    unnamed x9, local copies, waits for them, and re-layouts  2.71 us
  transfers between devices with their start and end apart: 30, of which 17 were waited for; matrix products, arithmetic and copies ran while one was open for 2% of the time, Pallas kernels for 10%

profile of v1, /device:TPU:0, one launch (start us, length us, event | category | flops | bytes accessed | tf_op | source)
XLA Modules:
  0.0 106.4 jit_solution(9122617702549660883)
XLA Ops:
  3.5 7.0 %all-to-all-start = ((bf16[2,16,1664]{2,0,1:T(2,128)(2,1)}), bf16[2,16,1664]{2,0,1:T(2,128)(2,1)S(1)}, u32[]{:S(2)}, u32[]{:S(2)}) async-start(bf16[2,16,1664]{2,0,1:T(2,128)(2,1)} %copy.17), calls=%async_computation | async-start | bytes 212992 | tf_op jit(solution)/shard_map/all_to_all | solution.py:418
  10.6 1.8 %shard_map.142 = (bf16[2,128,256]{2,1,0:T(8,128)(2,1)S(1)}, bf16[2,128,256]{2,1,0:T(8,128)(2,1)}, bf16[2,128,256]{2,1,0:T(8,128)(2,1)S(1)}, bf16[2,128,256]{2,1,0:T(8,128)(2,1)S(1)}) custom-call(s32[1]{0:T(128)} %bitcast.at_ref, bf16[128,2048]{1,0:T(8,128)(2,1)} %weight_hbm.1), custom_call_target="tpu_custom_call" | custom-call | bytes 1048576 | tf_op jit(solution)/shard_map/pallas_call | solution.py:30
  13.7 1.9 %collective-permute-start.10 = (bf16[2,128,256]{2,1,0:T(8,128)(2,1)}, bf16[2,128,256]{2,1,0:T(8,128)(2,1)S(1)}, u32[]{:S(2)}, u32[]{:S(2)}) collective-permute-start(bf16[2,128,256]{2,1,0:T(8,128)(2,1)} %get-tuple-element.22), channel_id=1, source_target_pairs={{0,4},{1,5},{2,6},{3,7},{4,0},{5,1},{6,2},{7,3},{8,12},{9,13},{10,... | collective-permute-start | bytes 393224 | tf_op jit(solution)/shard_map/ppermute | solution.py:359
  16.4 1.8 %all-to-all-done = bf16[2,16,1664]{2,0,1:T(2,128)(2,1)S(1)} async-done(((bf16[2,16,1664]{2,0,1:T(2,128)(2,1)}), bf16[2,16,1664]{2,0,1:T(2,128)(2,1)S(1)}, u32[]{:S(2)}, u32[]{:S(2)}) %all-to-all-start) | async-done | bytes 106528 | tf_op jit(solution)/shard_map/all_to_all | solution.py:418
  19.7 2.6 %shard_map.141 = (bf16[16,1024]{1,0:T(8,128)(2,1)S(1)}, bf16[16,1024]{1,0:T(8,128)(2,1)S(1)}) custom-call(s32[1]{0:T(128)} %bitcast.at_ref, bf16[32,1664]{1,0:T(8,128)(2,1)S(1)} %reshape.28.row_ref, s32[32,8]{1,0:T(8,128)S(1)} %copy.18.length_ref, bf16[2048,128]{1,0:T(8,128)(2,1)} %bitcast.14, bf16[2048,128]{1,0:T(8,128)(2,1)} %bitcast.15), custom_call_target="tpu_custom_call" | custom-call | flops 268435456 | bytes 1048576 | tf_op jit(solution)/shard_map/pallas_call | solution.py:30
  22.4 1.7 %collective-permute-start.11 = (bf16[2,128,256]{2,1,0:T(8,128)(2,1)}, bf16[2,128,256]{2,1,0:T(8,128)(2,1)S(1)}, u32[]{:S(2)}, u32[]{:S(2)}) collective-permute-start(bf16[2,128,256]{2,1,0:T(8,128)(2,1)} %copy-done.1), channel_id=1, source_target_pairs={{0,8},{1,9},{2,10},{3,11},{4,12},{5,13},{6,14},{7,15},{8,0},{9,1},... | collective-permute-start | bytes 393224 | tf_op jit(solution)/shard_map/ppermute | solution.py:359
  24.1 2.1 %collective-permute-start.12 = (bf16[2,128,256]{2,1,0:T(8,128)(2,1)}, bf16[2,128,256]{2,1,0:T(8,128)(2,1)S(1)}, u32[]{:S(2)}, u32[]{:S(2)}) collective-permute-start(bf16[2,128,256]{2,1,0:T(8,128)(2,1)} %copy-done), channel_id=1, source_target_pairs={{0,12},{1,13},{2,14},{3,15},{4,8},{5,9},{6,10},{7,11},{8,4},{9,5},... | collective-permute-start | bytes 393224 | tf_op jit(solution)/shard_map/ppermute | solution.py:359
  26.2 8.9 %collective-permute-done.11.refs_2_ = bf16[2,128,256]{2,1,0:T(8,128)(2,1)S(1)} collective-permute-done((bf16[2,128,256]{2,1,0:T(8,128)(2,1)}, bf16[2,128,256]{2,1,0:T(8,128)(2,1)S(1)}, u32[]{:S(2)}, u32[]{:S(2)}) %collective-permute-start.11) | collective-permute-done | bytes 131104 | tf_op jit(solution)/shard_map/ppermute | solution.py:359
  35.2 2.4 %collective-permute-start.8 = (bf16[2,16,1024]{2,1,0:T(8,128)(2,1)S(1)}, bf16[2,16,1024]{2,1,0:T(8,128)(2,1)S(1)}, u32[]{:S(2)}, u32[]{:S(2)}) collective-permute-start(bf16[2,16,1024]{2,1,0:T(8,128)(2,1)S(1)} %pad_maximum_fusion.refs_4_.refs_0_), channel_id=1, source_target_pairs={{0,12},{1,13},{2,14},{3,15},{4,8},{5,9},{6,10},{7,11},{8,4},{9,5},... | collective-permute-start | bytes 196616 | tf_op jit(solution)/shard_map/ppermute | solution.py:359
  37.6 1.9 %collective-permute-start.6 = (bf16[2,16,1024]{2,1,0:T(8,128)(2,1)S(1)}, bf16[2,16,1024]{2,1,0:T(8,128)(2,1)S(1)}, u32[]{:S(2)}, u32[]{:S(2)}) collective-permute-start(bf16[2,16,1024]{2,1,0:T(8,128)(2,1)S(1)} %pad_maximum_fusion.refs_4_.refs_0_), channel_id=1, source_target_pairs={{0,8},{1,9},{2,10},{3,11},{4,12},{5,13},{6,14},{7,15},{8,0},{9,1},... | collective-permute-start | bytes 196616 | tf_op jit(solution)/shard_map/ppermute | solution.py:359
  39.5 1.8 %collective-permute-done.8.refs_6_ = bf16[2,16,1024]{2,1,0:T(8,128)(2,1)S(1)} collective-permute-done((bf16[2,16,1024]{2,1,0:T(8,128)(2,1)S(1)}, bf16[2,16,1024]{2,1,0:T(8,128)(2,1)S(1)}, u32[]{:S(2)}, u32[]{:S(2)}) %collective-permute-start.8) | collective-permute-done | bytes 65568 | tf_op jit(solution)/shard_map/ppermute | solution.py:359
  41.3 2.8 %collective-permute-done.6.refs_4_ = bf16[2,16,1024]{2,1,0:T(8,128)(2,1)S(1)} collective-permute-done((bf16[2,16,1024]{2,1,0:T(8,128)(2,1)S(1)}, bf16[2,16,1024]{2,1,0:T(8,128)(2,1)S(1)}, u32[]{:S(2)}, u32[]{:S(2)}) %collective-permute-start.6) | collective-permute-done | bytes 65568 | tf_op jit(solution)/shard_map/ppermute | solution.py:359
  46.6 2.5 %collective-permute-done.3.refs_1_ = bf16[2,16,1024]{2,1,0:T(8,128)(2,1)S(1)} collective-permute-done((bf16[2,16,1024]{2,1,0:T(8,128)(2,1)S(1)}, bf16[2,16,1024]{2,1,0:T(8,128)(2,1)S(1)}, u32[]{:S(2)}, u32[]{:S(2)}) %collective-permute-start.3) | collective-permute-done | bytes 65568 | tf_op jit(solution)/shard_map/ppermute | solution.py:359
  50.1 5.1 %collective-permute-done.9.refs_7_ = bf16[2,16,1024]{2,1,0:T(8,128)(2,1)S(1)} collective-permute-done((bf16[2,16,1024]{2,1,0:T(8,128)(2,1)S(1)}, bf16[2,16,1024]{2,1,0:T(8,128)(2,1)S(1)}, u32[]{:S(2)}, u32[]{:S(2)}) %collective-permute-start.9) | collective-permute-done | bytes 65568 | tf_op jit(solution)/shard_map/ppermute | solution.py:359
  56.2 3.2 %collective-permute-done.7.refs_5_ = bf16[2,16,1024]{2,1,0:T(8,128)(2,1)S(1)} collective-permute-done((bf16[2,16,1024]{2,1,0:T(8,128)(2,1)S(1)}, bf16[2,16,1024]{2,1,0:T(8,128)(2,1)S(1)}, u32[]{:S(2)}, u32[]{:S(2)}) %collective-permute-start.7) | collective-permute-done | bytes 65568 | tf_op jit(solution)/shard_map/ppermute | solution.py:359
  60.5 3.2 %collective-permute-done.5.refs_3_ = bf16[2,16,1024]{2,1,0:T(8,128)(2,1)S(1)} collective-permute-done((bf16[2,16,1024]{2,1,0:T(8,128)(2,1)S(1)}, bf16[2,16,1024]{2,1,0:T(8,128)(2,1)S(1)}, u32[]{:S(2)}, u32[]{:S(2)}) %collective-permute-start.5) | collective-permute-done | bytes 65568 | tf_op jit(solution)/shard_map/ppermute | solution.py:359
  66.2 1.8 %collective-permute-start.18 = (bf16[128,256]{1,0:T(8,128)(2,1)S(1)}, bf16[128,256]{1,0:T(8,128)(2,1)S(1)}, u32[]{:S(2)}, u32[]{:S(2)}) collective-permute-start(bf16[128,256]{1,0:T(8,128)(2,1)S(1)} %shard_map.144.refs_0_), channel_id=1, source_target_pairs={{0,12},{1,13},{2,14},{3,15},{4,8},{5,9},{6,10},{7,11},{8,4},{9,5},... | collective-permute-start | bytes 196616 | tf_op jit(solution)/shard_map/ppermute | solution.py:359
  68.0 5.0 %collective-permute-done.18.refs_3_ = bf16[128,256]{1,0:T(8,128)(2,1)S(1)} collective-permute-done((bf16[128,256]{1,0:T(8,128)(2,1)S(1)}, bf16[128,256]{1,0:T(8,128)(2,1)S(1)}, u32[]{:S(2)}, u32[]{:S(2)}) %collective-permute-start.18) | collective-permute-done | bytes 65568 | tf_op jit(solution)/shard_map/ppermute | solution.py:359
  73.0 2.1 %collective-permute-done.17.refs_2_ = bf16[128,256]{1,0:T(8,128)(2,1)S(1)} collective-permute-done((bf16[128,256]{1,0:T(8,128)(2,1)S(1)}, bf16[128,256]{1,0:T(8,128)(2,1)S(1)}, u32[]{:S(2)}, u32[]{:S(2)}) %collective-permute-start.17) | collective-permute-done | bytes 65568 | tf_op jit(solution)/shard_map/ppermute | solution.py:359
  80.3 5.1 %shard_map.145.partial_ref = f32[8,128,384]{2,1,0:T(8,128)S(1)} custom-call(s32[1]{0:T(128)} %bitcast.at_ref, bf16[1,2048]{1,0:T(2,128)(2,1)S(1)} %reshape.27.gain_ref, bf16[2,2048,384]{2,1,0:T(8,128)(2,1)S(1)} %collective-permute-done.gate_ref, bf16[2,2048,384]{2,1,0:T(8,128)(2,1)} %collective-permute-done.1.up_ref, bf16[2,2048,384]{2,1,0:T(8,128)(2,1)} %gate_hbm.3, ...), custom_call_target="tpu_custom_call" | custom-call | flops 805306368 | bytes 6291456 | tf_op jit(solution)/shard_map/pallas_call | solution.py:30
  85.4 7.7 %shard_map.146 = (bf16[16,2048]{1,0:T(8,128)(2,1)}, bf16[2,16,2048]{2,1,0:T(8,128)(2,1)S(1)}, bf16[2,16,2048]{2,1,0:T(8,128)(2,1)S(1)}, bf16[2,16,2048]{2,1,0:T(8,128)(2,1)S(1)}, bf16[2,16,2048]{2,1,0:T(8,128)(2,1)S(1)}) custom-call(s32[1]{0:T(128)} %bitcast.at_ref, bf16[1,2048]{1,0:T(2,128)(2,1)S(1)} %reshape.27.gain_ref, ...), custom_call_target="tpu_custom_call" | custom-call | flops 1610612736 | bytes 12582912 | tf_op jit(solution)/shard_map/pallas_call | solution.py:30
  95.2 2.9 %collective-permute-done.24.piece_ref = bf16[2,16,2048]{2,1,0:T(8,128)(2,1)S(1)} collective-permute-done((bf16[2,16,2048]{2,1,0:T(8,128)(2,1)S(1)}, bf16[2,16,2048]{2,1,0:T(8,128)(2,1)S(1)}, u32[]{:S(2)}, u32[]{:S(2)}) %collective-permute-start.24) | collective-permute-done | bytes 131104 | tf_op jit(solution)/shard_map/ppermute | solution.py:359
  98.2 2.3 %collective-permute-start.25 = (bf16[16,2048]{1,0:T(8,128)(2,1)S(1)}, bf16[16,2048]{1,0:T(8,128)(2,1)S(1)}, u32[]{:S(2)}, u32[]{:S(2)}) collective-permute-start(bf16[16,2048]{1,0:T(8,128)(2,1)S(1)} %get-tuple-element.30), channel_id=1, source_target_pairs={{0,12},{1,13},{2,14},{3,15},{4,8},{5,9},{6,10},{7,11},{8,4},{9,5},... | collective-permute-start | bytes 196616 | tf_op jit(solution)/shard_map/ppermute | solution.py:359
  100.6 2.2 %collective-permute-start.28 = (bf16[16,2048]{1,0:T(8,128)(2,1)S(1)}, bf16[16,2048]{1,0:T(8,128)(2,1)S(1)}, u32[]{:S(2)}, u32[]{:S(2)}) collective-permute-start(bf16[16,2048]{1,0:T(8,128)(2,1)S(1)} %get-tuple-element.34), channel_id=1, source_target_pairs={{0,4},{1,5},{2,6},{3,7},{4,0},{5,1},{6,2},{7,3},{8,12},{9,13},{10,... | collective-permute-start | bytes 196616 | tf_op jit(solution)/shard_map/ppermute | solution.py:359
  (60 shorter events, 25.6 us)
Async XLA Ops:
  0.6 77.6 %collective-permute-start = (bf16[2,2048,384]{2,1,0:T(8,128)(2,1)}, bf16[2,2048,384]{2,1,0:T(8,128)(2,1)S(1)}, u32[]{:S(2)}, u32[]{:S(2)}) collective-permute-start(bf16[2,2048,384]{2,1,0:T(8,128)(2,1)} %gate_hbm.3), channel_id=1, source_target_pairs={{0,1},{1,0},{2,3},{3,2},{4,5},{5,4},{6,7},{7,6},{8,9},{9,8},{10,11... | collective-permute-start | bytes 9437192 | tf_op jit(solution)/shard_map/ppermute | solution.py:359
  1.2 78.1 %collective-permute-start.1 = (bf16[2,2048,384]{2,1,0:T(8,128)(2,1)}, bf16[2,2048,384]{2,1,0:T(8,128)(2,1)}, u32[]{:S(2)}, u32[]{:S(2)}) collective-permute-start(bf16[2,2048,384]{2,1,0:T(8,128)(2,1)} %up_hbm.3), channel_id=1, source_target_pairs={{0,1},{1,0},{2,3},{3,2},{4,5},{5,4},{6,7},{7,6},{8,9},{9,8},{10,11... | collective-permute-start | bytes 9437192 | tf_op jit(solution)/shard_map/ppermute | solution.py:359
  1.3 84.1 %collective-permute-start.19 = (bf16[2,384,2048]{2,1,0:T(8,128)(2,1)}, bf16[2,384,2048]{2,1,0:T(8,128)(2,1)}, u32[]{:S(2)}, u32[]{:S(2)}) collective-permute-start(bf16[2,384,2048]{2,1,0:T(8,128)(2,1)} %down_hbm.1), channel_id=1, source_target_pairs={{0,1},{1,0},{2,3},{3,2},{4,5},{5,4},{6,7},{7,6},{8,9},{9,8},{10,11... | collective-permute-start | bytes 9437192 | tf_op jit(solution)/shard_map/ppermute | solution.py:359
  3.5 14.7 %all-to-all-start = ((bf16[2,16,1664]{2,0,1:T(2,128)(2,1)}), bf16[2,16,1664]{2,0,1:T(2,128)(2,1)S(1)}, u32[]{:S(2)}, u32[]{:S(2)}) async-start(bf16[2,16,1664]{2,0,1:T(2,128)(2,1)} %copy.17), calls=%async_computation | async-start | bytes 212992 | tf_op jit(solution)/shard_map/all_to_all | solution.py:418
  13.7 8.7 %collective-permute-start.10 = (bf16[2,128,256]{2,1,0:T(8,128)(2,1)}, bf16[2,128,256]{2,1,0:T(8,128)(2,1)S(1)}, u32[]{:S(2)}, u32[]{:S(2)}) collective-permute-start(bf16[2,128,256]{2,1,0:T(8,128)(2,1)} %get-tuple-element.22), channel_id=1, source_target_pairs={{0,4},{1,5},{2,6},{3,7},{4,0},{5,1},{6,2},{7,3},{8,12},{9,13},{10,... | collective-permute-start | bytes 393224 | tf_op jit(solution)/shard_map/ppermute | solution.py:359
  22.4 12.8 %collective-permute-start.11 = (bf16[2,128,256]{2,1,0:T(8,128)(2,1)}, bf16[2,128,256]{2,1,0:T(8,128)(2,1)S(1)}, u32[]{:S(2)}, u32[]{:S(2)}) collective-permute-start(bf16[2,128,256]{2,1,0:T(8,128)(2,1)} %copy-done.1), channel_id=1, source_target_pairs={{0,8},{1,9},{2,10},{3,11},{4,12},{5,13},{6,14},{7,15},{8,0},{9,1},... | collective-permute-start | bytes 393224 | tf_op jit(solution)/shard_map/ppermute | solution.py:359
  24.1 13.5 %collective-permute-start.12 = (bf16[2,128,256]{2,1,0:T(8,128)(2,1)}, bf16[2,128,256]{2,1,0:T(8,128)(2,1)S(1)}, u32[]{:S(2)}, u32[]{:S(2)}) collective-permute-start(bf16[2,128,256]{2,1,0:T(8,128)(2,1)} %copy-done), channel_id=1, source_target_pairs={{0,12},{1,13},{2,14},{3,15},{4,8},{5,9},{6,10},{7,11},{8,4},{9,5},... | collective-permute-start | bytes 393224 | tf_op jit(solution)/shard_map/ppermute | solution.py:359
  35.2 6.1 %collective-permute-start.8 = (bf16[2,16,1024]{2,1,0:T(8,128)(2,1)S(1)}, bf16[2,16,1024]{2,1,0:T(8,128)(2,1)S(1)}, u32[]{:S(2)}, u32[]{:S(2)}) collective-permute-start(bf16[2,16,1024]{2,1,0:T(8,128)(2,1)S(1)} %pad_maximum_fusion.refs_4_.refs_0_), channel_id=1, source_target_pairs={{0,12},{1,13},{2,14},{3,15},{4,8},{5,9},{6,10},{7,11},{8,4},{9,5},... | collective-permute-start | bytes 196616 | tf_op jit(solution)/shard_map/ppermute | solution.py:359
  37.6 6.5 %collective-permute-start.6 = (bf16[2,16,1024]{2,1,0:T(8,128)(2,1)S(1)}, bf16[2,16,1024]{2,1,0:T(8,128)(2,1)S(1)}, u32[]{:S(2)}, u32[]{:S(2)}) collective-permute-start(bf16[2,16,1024]{2,1,0:T(8,128)(2,1)S(1)} %pad_maximum_fusion.refs_4_.refs_0_), channel_id=1, source_target_pairs={{0,8},{1,9},{2,10},{3,11},{4,12},{5,13},{6,14},{7,15},{8,0},{9,1},... | collective-permute-start | bytes 196616 | tf_op jit(solution)/shard_map/ppermute | solution.py:359
  41.3 4.3 %collective-permute-start.4 = (bf16[2,16,1024]{2,1,0:T(8,128)(2,1)S(1)}, bf16[2,16,1024]{2,1,0:T(8,128)(2,1)S(1)}, u32[]{:S(2)}, u32[]{:S(2)}) collective-permute-start(bf16[2,16,1024]{2,1,0:T(8,128)(2,1)S(1)} %pad_maximum_fusion.refs_4_.refs_0_), channel_id=1, source_target_pairs={{0,4},{1,5},{2,6},{3,7},{4,0},{5,1},{6,2},{7,3},{8,12},{9,13},{10,... | collective-permute-start | bytes 196616 | tf_op jit(solution)/shard_map/ppermute | solution.py:359
  44.1 5.0 %collective-permute-start.3 = (bf16[2,16,1024]{2,1,0:T(8,128)(2,1)S(1)}, bf16[2,16,1024]{2,1,0:T(8,128)(2,1)S(1)}, u32[]{:S(2)}, u32[]{:S(2)}) collective-permute-start(bf16[2,16,1024]{2,1,0:T(8,128)(2,1)S(1)} %pad_maximum_fusion.refs_4_.refs_0_), channel_id=1, source_target_pairs={{0,2},{1,3},{2,0},{3,1},{4,6},{5,7},{6,4},{7,5},{8,10},{9,11},{10,... | collective-permute-start | bytes 196616 | tf_op jit(solution)/shard_map/ppermute | solution.py:359
  45.5 18.2 %collective-permute-start.14 = (bf16[4,128,256]{2,1,0:T(8,128)(2,1)S(1)}, bf16[4,128,256]{2,1,0:T(8,128)(2,1)S(1)}, u32[]{:S(2)}, u32[]{:S(2)}) collective-permute-start(bf16[4,128,256]{2,1,0:T(8,128)(2,1)S(1)} %get-tuple-element.26), channel_id=1, source_target_pairs={{0,2},{1,3},{2,0},{3,1},{4,6},{5,7},{6,4},{7,5},{8,10},{9,11},{10,... | collective-permute-start | bytes 786440 | tf_op jit(solution)/shard_map/ppermute | solution.py:359
  49.1 6.1 %collective-permute-start.9 = (bf16[2,16,1024]{2,1,0:T(8,128)(2,1)S(1)}, bf16[2,16,1024]{2,1,0:T(8,128)(2,1)S(1)}, u32[]{:S(2)}, u32[]{:S(2)}) collective-permute-start(bf16[2,16,1024]{2,1,0:T(8,128)(2,1)S(1)} %collective-permute-done.8.refs_6_), channel_id=1, source_target_pairs={{0,2},{1,3},{2,0},{3,1},{4,6},{5,7},{6,4},{7,5},{8,10},{9,11},{10,... | collective-permute-start | bytes 196616 | tf_op jit(solution)/shard_map/ppermute | solution.py:359
  66.2 6.8 %collective-permute-start.18 = (bf16[128,256]{1,0:T(8,128)(2,1)S(1)}, bf16[128,256]{1,0:T(8,128)(2,1)S(1)}, u32[]{:S(2)}, u32[]{:S(2)}) collective-permute-start(bf16[128,256]{1,0:T(8,128)(2,1)S(1)} %shard_map.144.refs_0_), channel_id=1, source_target_pairs={{0,12},{1,13},{2,14},{3,15},{4,8},{5,9},{6,10},{7,11},{8,4},{9,5},... | collective-permute-start | bytes 196616 | tf_op jit(solution)/shard_map/ppermute | solution.py:359
  68.0 7.1 %collective-permute-start.17 = (bf16[128,256]{1,0:T(8,128)(2,1)S(1)}, bf16[128,256]{1,0:T(8,128)(2,1)S(1)}, u32[]{:S(2)}, u32[]{:S(2)}) collective-permute-start(bf16[128,256]{1,0:T(8,128)(2,1)S(1)} %shard_map.144.refs_0_), channel_id=1, source_target_pairs={{0,8},{1,9},{2,10},{3,11},{4,12},{5,13},{6,14},{7,15},{8,0},{9,1},... | collective-permute-start | bytes 196616 | tf_op jit(solution)/shard_map/ppermute | solution.py:359
  75.1 10.3 %collective-permute-start.20 = (bf16[128,256]{1,0:T(8,128)(2,1)S(1)}, bf16[128,256]{1,0:T(8,128)(2,1)S(1)}, u32[]{:S(2)}, u32[]{:S(2)}) collective-permute-start(bf16[128,256]{1,0:T(8,128)(2,1)S(1)} %shard_map.144.refs_0_), channel_id=1, source_target_pairs={{0,2},{1,3},{2,0},{3,1},{4,6},{5,7},{6,4},{7,5},{8,10},{9,11},{10,... | collective-permute-start | bytes 196616 | tf_op jit(solution)/shard_map/ppermute | solution.py:359
  77.2 8.1 %collective-permute-start.23 = (bf16[128,256]{1,0:T(8,128)(2,1)S(1)}, bf16[128,256]{1,0:T(8,128)(2,1)S(1)}, u32[]{:S(2)}, u32[]{:S(2)}) collective-permute-start(bf16[128,256]{1,0:T(8,128)(2,1)S(1)} %collective-permute-done.18.refs_3_), channel_id=1, source_target_pairs={{0,2},{1,3},{2,0},{3,1},{4,6},{5,7},{6,4},{7,5},{8,10},{9,11},{10,... | collective-permute-start | bytes 196616 | tf_op jit(solution)/shard_map/ppermute | solution.py:359
  78.3 7.1 %collective-permute-start.22 = (bf16[128,256]{1,0:T(8,128)(2,1)S(1)}, bf16[128,256]{1,0:T(8,128)(2,1)S(1)}, u32[]{:S(2)}, u32[]{:S(2)}) collective-permute-start(bf16[128,256]{1,0:T(8,128)(2,1)S(1)} %collective-permute-done.17.refs_2_), channel_id=1, source_target_pairs={{0,2},{1,3},{2,0},{3,1},{4,6},{5,7},{6,4},{7,5},{8,10},{9,11},{10,... | collective-permute-start | bytes 196616 | tf_op jit(solution)/shard_map/ppermute | solution.py:359
  79.3 6.1 %collective-permute-start.21 = (bf16[128,256]{1,0:T(8,128)(2,1)S(1)}, bf16[128,256]{1,0:T(8,128)(2,1)S(1)}, u32[]{:S(2)}, u32[]{:S(2)}) collective-permute-start(bf16[128,256]{1,0:T(8,128)(2,1)S(1)} %collective-permute-done.16.refs_1_), channel_id=1, source_target_pairs={{0,2},{1,3},{2,0},{3,1},{4,6},{5,7},{6,4},{7,5},{8,10},{9,11},{10,... | collective-permute-start | bytes 196616 | tf_op jit(solution)/shard_map/ppermute | solution.py:359
  93.1 5.0 %collective-permute-start.24 = (bf16[2,16,2048]{2,1,0:T(8,128)(2,1)S(1)}, bf16[2,16,2048]{2,1,0:T(8,128)(2,1)S(1)}, u32[]{:S(2)}, u32[]{:S(2)}) collective-permute-start(bf16[2,16,2048]{2,1,0:T(8,128)(2,1)S(1)} %get-tuple-element.29), channel_id=1, source_target_pairs={{0,2},{1,3},{2,0},{3,1},{4,6},{5,7},{6,4},{7,5},{8,10},{9,11},{10,... | collective-permute-start | bytes 393224 | tf_op jit(solution)/shard_map/ppermute | solution.py:359
  94.2 6.4 %collective-permute-start.27 = (bf16[2,16,2048]{2,1,0:T(8,128)(2,1)S(1)}, bf16[2,16,2048]{2,1,0:T(8,128)(2,1)S(1)}, u32[]{:S(2)}, u32[]{:S(2)}) collective-permute-start(bf16[2,16,2048]{2,1,0:T(8,128)(2,1)S(1)} %get-tuple-element.33), channel_id=1, source_target_pairs={{0,2},{1,3},{2,0},{3,1},{4,6},{5,7},{6,4},{7,5},{8,10},{9,11},{10,... | collective-permute-start | bytes 393224 | tf_op jit(solution)/shard_map/ppermute | solution.py:359
  98.2 6.1 %collective-permute-start.25 = (bf16[16,2048]{1,0:T(8,128)(2,1)S(1)}, bf16[16,2048]{1,0:T(8,128)(2,1)S(1)}, u32[]{:S(2)}, u32[]{:S(2)}) collective-permute-start(bf16[16,2048]{1,0:T(8,128)(2,1)S(1)} %get-tuple-element.30), channel_id=1, source_target_pairs={{0,12},{1,13},{2,14},{3,15},{4,8},{5,9},{6,10},{7,11},{8,4},{9,5},... | collective-permute-start | bytes 196616 | tf_op jit(solution)/shard_map/ppermute | solution.py:359
  100.5 5.2 %collective-permute-start.26 = (bf16[16,2048]{1,0:T(8,128)(2,1)S(1)}, bf16[16,2048]{1,0:T(8,128)(2,1)S(1)}, u32[]{:S(2)}, u32[]{:S(2)}) collective-permute-start(bf16[16,2048]{1,0:T(8,128)(2,1)S(1)} %get-tuple-element.31), channel_id=1, source_target_pairs={{0,8},{1,9},{2,10},{3,11},{4,12},{5,13},{6,14},{7,15},{8,0},{9,1},... | collective-permute-start | bytes 196616 | tf_op jit(solution)/shard_map/ppermute | solution.py:359
  100.6 5.1 %collective-permute-start.28 = (bf16[16,2048]{1,0:T(8,128)(2,1)S(1)}, bf16[16,2048]{1,0:T(8,128)(2,1)S(1)}, u32[]{:S(2)}, u32[]{:S(2)}) collective-permute-start(bf16[16,2048]{1,0:T(8,128)(2,1)S(1)} %get-tuple-element.34), channel_id=1, source_target_pairs={{0,4},{1,5},{2,6},{3,7},{4,0},{5,1},{6,2},{7,3},{8,12},{9,13},{10,... | collective-permute-start | bytes 196616 | tf_op jit(solution)/shard_map/ppermute | solution.py:359
  (10 other events, 92.3 us)

commit v2 on v1

--- a/solution.py
+++ b/solution.py
@@ -57,17 +57,30 @@
     value_hbm,
     id_hbm,
     share_hbm,
+    length_hbm,
+    at_ref,
     out_ref,
+    seen_ref,
     query_ref,
     key_ref,
     value_ref,
     id_ref,
     share_ref,
+    length_ref,
     sems,
 ):
-    refs = (id_ref, share_ref, query_ref, key_ref, value_ref)
-    for copy in fetch((id_hbm, share_hbm, query_hbm, key_hbm, value_hbm), refs, sems):
+    refs = (id_ref, share_ref, length_ref, query_ref, key_ref, value_ref)
+    sources = (id_hbm, share_hbm, length_hbm, query_hbm, key_hbm, value_hbm)
+    for copy in fetch(sources, refs, sems):
         copy.wait()
+    new = length_ref.shape[1]
+    member = at_ref[0] // KVH
+    mine = jnp.where(iota(length_ref.shape, 0) == member, length_ref[...], 0).astype(jnp.float32)
+    mine = jnp.broadcast_to(jnp.sum(mine, axis=0, keepdims=True), (new, new))
+    mine = jnp.sum(
+        jnp.where(iota((new, new), 0) == iota((new, new), 1), mine, 0.0), axis=1, keepdims=True
+    )
+    seen_ref[...] = jnp.broadcast_to(mine, seen_ref.shape).astype(jnp.int32)
     per_rows, count, wide = query_ref.shape
     members = id_ref.shape[1]
     width = (out_ref.shape[2] - wide - 2 * HD) // 3
@@ -93,14 +106,15 @@
             at += width
 
 
-def split_kernel(at_ref, weight_hbm, *refs):
+def split_kernel(at_ref, group_ref, weight_hbm, *refs):
     parts, sems = refs[:-1], refs[-1]
     chip = at_ref[0] // 2
     sources, targets = [], []
     for k, part in reversed(list(enumerate(parts))):
         for y in range(2):
             start = pl.multiple_of((chip ^ (2 * k + y)) * part.shape[2], LANES)
-            sources.append(weight_hbm.at[:, pl.ds(start, part.shape[2])])
+            rows = pl.ds(pl.multiple_of(group_ref[0] * part.shape[1], 16), part.shape[1])
+            sources.append(weight_hbm.at[rows, pl.ds(start, part.shape[2])])
             targets.append(part.at[y])
     for copy in fetch(sources, targets, sems):
         copy.wait()
@@ -136,12 +150,7 @@
     wide = heads * HD
     cached = key_ref.shape[0]
     step = math.gcd(cached, 512)
-    member = at_ref[0] // KVH
-    length = jnp.sum(
-        jnp.where(iota(length_ref.shape, 1) == member, length_ref[...], 0).astype(jnp.float32),
-        axis=1,
-        keepdims=True,
-    ).astype(jnp.int32)
+    length = length_ref[:, :1]
     lengths = jnp.concatenate([length] * heads, axis=0)
     query = jnp.concatenate([row_ref[:, h * HD : (h + 1) * HD] for h in range(heads)], axis=0)
     rows = heads * new
@@ -198,17 +207,17 @@
     send_ref[...] = result[half:]
 
 
-def project_kernel(at_ref, *refs):
-    pieces, columns, (out_ref, weight_ref) = refs[:-6], refs[-6:-2], refs[-2:]
+def project_kernel(at_ref, group_ref, *refs):
+    pieces, columns, (out_ref, weight_ref) = refs[:-10], refs[-10:-2], refs[-2:]
     me = at_ref[0]
     members = len(pieces)
     _, places, wide = pieces[0].shape
     rows = members * places
-    owned = columns[0].shape[1]
+    part = columns[0].shape[1]
     for i, ref in enumerate(columns):
         for k in range(ref.shape[0]):
-            head = me ^ (4 * k + i)
-            weight_ref[pl.ds(pl.multiple_of(head * owned, owned), owned), :] = ref[k]
+            place = 2 * (me ^ (4 * k + i // 2)) + (group_ref[0] ^ (i % 2))
+            weight_ref[pl.ds(pl.multiple_of(place * part, part), part), :] = ref[k]
     total = jnp.zeros(out_ref.shape, jnp.float32)
     for half in range(KVH):
         start = pl.multiple_of((me ^ half) % KVH * wide, wide)
@@ -227,7 +236,7 @@
 
 def weigh(chip, odd, pieces, gain_ref, there, own_hbm, own_ref, sems):
     lanes = pieces[0].shape[1]
-    experts = own_ref.shape[2]
+    experts = own_ref.shape[1]
     starts = [
         pl.multiple_of((chip ^ (2 * i + odd)) * lanes, lanes) for i in range(len(pieces))
     ]
@@ -235,29 +244,37 @@
     for i, start in enumerate(starts):
         for m, source in enumerate(own_hbm):
             sources.append(source.at[:, pl.ds(start, lanes), :])
-            targets.append(own_ref.at[m, i])
+            targets.append(own_ref.at[m, :, pl.ds(i * lanes, lanes), :])
     copies = fetch(sources, targets, sems)
-    rows = [
-        (
-            piece[...].astype(jnp.float32) * gain_ref[:, pl.ds(start, lanes)].astype(jnp.float32)
-        ).astype(jnp.bfloat16)
-        for piece, start in zip(pieces, starts)
-    ]
+    rows = jnp.concatenate(
+        [
+            (
+                piece[...].astype(jnp.float32)
+                * gain_ref[:, pl.ds(start, lanes)].astype(jnp.float32)
+            ).astype(jnp.bfloat16)
+            for piece, start in zip(pieces, starts)
+        ],
+        axis=1,
+    )
 
     def products(pick):
         return [
-            sum(
-                jnp.dot(row, pick(m, i, e), preferred_element_type=jnp.float32)
-                for i, row in enumerate(rows)
+            jnp.dot(
+                rows,
+                jnp.concatenate([pick(0, e), pick(1, e)], axis=1),
+                preferred_element_type=jnp.float32,
             )
             for e in range(experts)
-            for m in range(2)
         ]
 
-    out = products(lambda m, i, e: there[m][e, pl.ds(starts[i], lanes), :])
+    out = products(
+        lambda m, e: jnp.concatenate(
+            [there[m][e, pl.ds(start, lanes), :] for start in starts], axis=0
+        )
+    )
     for copy in copies:
         copy.wait()
-    return out + products(lambda m, i, e: own_ref[m, i, e])
+    return out + products(lambda m, e: own_ref[m, e])
 
 
 def gate_kernel(at_ref, gain_ref, gate_ref, up_ref, gate_hbm, up_hbm, *refs):
@@ -290,7 +307,7 @@
     *refs,
 ):
     near, far, projected_ref = refs[: chips // 2], refs[chips // 2 : chips], refs[chips]
-    outs, (result_ref, own_ref, down_own_ref, sems, down_sems) = refs[chips + 1 : -5], refs[-5:]
+    outs, (result_ref, own_ref, sems) = refs[chips + 1 : -3], refs[-3:]
     me = at_ref[0]
     chip, core = me // 2, me % 2
     rows, lanes = near[0].shape
@@ -318,7 +335,6 @@
     share = jnp.where(mine, info[:, width : 2 * width] + info[:, 2 * width :], 0.0)
     whole = jnp.sum(share, axis=1, keepdims=True)
 
-    (copy,) = fetch((down_hbm,), (down_own_ref,), down_sems)
     out = weigh(
         chip, 1, far, gain_ref, (gate_ref, up_ref), (gate_hbm, up_hbm), own_ref, sems
     )
@@ -327,17 +343,17 @@
         device = me ^ (1 - d // experts)
         chosen = info[:, :width] == (device * experts + d % experts).astype(jnp.float32)
         scale = jnp.sum(jnp.where(chosen, share, 0.0), axis=1, keepdims=True) / whole
-        gate = (partial_ref[2 * d] + out[2 * d]) * inverse
-        up = (partial_ref[2 * d + 1] + out[2 * d + 1]) * inverse
+        both = (partial_ref[d] + out[d]) * inverse
+        gate, up = both[:, : both.shape[1] // 2], both[:, both.shape[1] // 2 :]
         hidden.append((gate / (1.0 + jnp.exp(-gate)) * up * scale).astype(jnp.bfloat16))
-    copy.wait()
     step = 512
     for at in range(0, down_ref.shape[2], step):
         part = jnp.zeros((rows, step), jnp.float32)
-        for d, value in enumerate(hidden):
-            ref = (down_ref, down_own_ref)[d // experts]
+        for d, ref in enumerate((down_ref, down_hbm)):
             part = part + jnp.dot(
-                value, ref[d % experts, :, at : at + step], preferred_element_type=jnp.float32
+                jnp.concatenate(hidden[d * experts : (d + 1) * experts], axis=1),
+                ref[:, :, at : at + step].reshape(-1, step),
+                preferred_element_type=jnp.float32,
             )
         result_ref[:, at : at + step] = part.astype(jnp.bfloat16)
     order = iter(block_order(chips))
@@ -354,9 +370,20 @@
         ).astype(jnp.bfloat16)
 
 
+def sum_kernel(*refs):
+    total = refs[0][...].astype(jnp.float32)
+    for ref in refs[1:-1]:
+        total = total + ref[...].astype(jnp.float32)
+    refs[-1][...] = total.astype(jnp.bfloat16)
+
+
 def swap(value, offset):
     count = lax.axis_size("seq")
     return lax.ppermute(value, "seq", [(i, i ^ offset) for i in range(count)])
+
+
+def cross(value):
+    return lax.ppermute(value, "groups", [(0, 1), (1, 0)])
 
 
 def scatter_pieces(far, near):
@@ -401,19 +428,20 @@
     per_dev = per_rows * members
     rows = per_dev * count
     at = lax.axis_index("seq").astype(jnp.int32).reshape(1)
+    group = lax.axis_index("groups").astype(jnp.int32).reshape(1)
     width = -(-members * TOPK // LANES) * LANES
     wide = QH // KVH * HD
     bf16 = jnp.bfloat16
-    (sent,) = call(
+    loads = (queries, keys, values, expert_ids, route_weights, cache_len.T)
+    sent, seen = call(
         pack_kernel,
-        [((per_rows, count, wide + 2 * HD + 3 * width), bf16)],
-        (queries, keys, values, expert_ids, route_weights),
-        scratch=[
-            pltpu.VMEM(a.shape, a.dtype)
-            for a in (queries, keys, values, expert_ids, route_weights)
-        ]
-        + [pltpu.SemaphoreType.DMA((5,))],
-        far=range(5),
+        [
+            ((per_rows, count, wide + 2 * HD + 3 * width), bf16),
+            ((new, LANES), jnp.int32),
+        ],
+        (*loads, at),
+        scratch=[pltpu.VMEM(a.shape, a.dtype) for a in loads] + [pltpu.SemaphoreType.DMA((6,))],
+        far=range(6),
     )
     taken = lax.all_to_all(sent, "seq", split_axis=1, concat_axis=0, tiled=True)
     taken = taken.reshape(new, sent.shape[2])
@@ -424,10 +452,10 @@
     gate_peer, up_peer, down_peer = swap(w_gate, 1), swap(w_up, 1), swap(w_down, 1)
     parts = call(
         split_kernel,
-        [((2, owned, lanes), bf16)] * (chips // 2),
-        (at, out_weight),
+        [((2, owned // 2, lanes), bf16)] * (chips // 2),
+        (at, group, out_weight),
         scratch=[pltpu.SemaphoreType.DMA((chips,))],
-        far=(1,),
+        far=(2,),
         moved=4 * out_weight.size,
     )
     parts = [parts[0]] + [swap(parts[k], 4 * k) for k in range(len(parts) - 1, 0, -1)][::-1]
@@ -435,7 +463,7 @@
     keep, send = call(
         functools.partial(attend_kernel, per_rows),
         [((new // 2, wide), bf16)] * 2,
-        (at, taken, cache_len, cache_keys.reshape(cached, HD), cache_values.reshape(cached, HD)),
+        (at, taken, seen, cache_keys.reshape(cached, HD), cache_values.reshape(cached, HD)),
         scratch=[
             pltpu.VMEM((row_count, cached), jnp.float32),
             pltpu.VMEM((cached, HD), bf16),
@@ -452,17 +480,22 @@
     heads = [piece for pair in zip(near, far) for piece in pair]
     columns, across = call(
         regroup_kernel,
-        [((chips // 2, owned, lanes), bf16)] * 2,
+        [((chips // 2, owned // 2, lanes), bf16)] * 2,
         (*parts, own),
         loose=(len(parts),),
     )
     beyond = swap(across, 2)
-    beyond_peer = swap(beyond, 1)
+    columns_there = cross(columns)
+    beyond_there = cross(beyond)
+    blocks = [columns, columns_there]
+    blocks += [swap(block, 1) for block in blocks]
+    blocks += [beyond, beyond_there]
+    blocks += [swap(block, 1) for block in blocks[-2:]]
     half = rows // 2
     (projected,) = call(
         project_kernel,
         [((half, lanes), bf16)],
-        (at, *heads, columns, swap(columns, 1), beyond, beyond_peer),
+        (at, group, *heads, *blocks),
         scratch=[pltpu.VMEM((D, lanes), bf16)],
         flops=2 * half * D * lanes,
         moved=4 * half * D,
@@ -470,10 +503,10 @@
     near, far = gather_rows(projected)
     gain = norm_gain.reshape(1, D)
     experts, _, hidden = w_gate.shape
-    own_rows = pltpu.VMEM((2, chips // 2, experts, lanes, hidden), bf16)
+    own_rows = pltpu.VMEM((2, experts, D // 2, hidden), bf16)
     (partial,) = call(
         gate_kernel,
-        [((4 * experts, half, hidden), jnp.float32)],
+        [((2 * experts, half, 2 * hidden), jnp.float32)],
         (at, gain, gate_peer, up_peer, w_gate, w_up, *near),
         scratch=[own_rows, pltpu.SemaphoreType.DMA((chips,))],
         far=(4, 5),
@@ -501,28 +534,27 @@
         scratch=[
             pltpu.VMEM((half, D), bf16),
             own_rows,
-            pltpu.VMEM(w_down.shape, bf16),
             pltpu.SemaphoreType.DMA((chips,)),
-            pltpu.SemaphoreType.DMA((1,)),
         ],
-        far=(4, 5, 9),
+        far=(4, 5),
         vmem_mib=24,
         flops=8 * half * w_gate.size,
         moved=8 * w_gate.size,
     )
     pieces = scatter_pieces(blocks[: chips // 4], blocks[chips // 4 :])
-    mixed = sum(piece.astype(jnp.float32) for piece in pieces)
+    (mixed,) = call(sum_kernel, [((per_dev, D), bf16)], pieces)
     shape = (per_rows, members, D)
-    return (projected.reshape(shape), mixed.astype(jnp.bfloat16).reshape(shape))
+    return (projected.reshape(shape), mixed.reshape(shape))
 
 
 def fits(mesh, out_rows, positions, experts):
     count = mesh.shape["seq"]
     owned = out_rows // count
     per_dev = positions // count * (count // KVH)
+    pair = mesh.shape["groups"] == 2
     power = count & (count - 1) == 0 and count >= 8
     small = per_dev * count * D * 2 <= 2 << 20
-    return power and owned == HD == LANES and count * LANES == D and per_dev % 16 == 0 and positions % 16 == 0 and small and experts <= 256
+    return pair and power and owned == HD == LANES and count * LANES == D and per_dev % 16 == 0 and positions % 16 == 0 and small and experts <= 256
 
 
 def attend(query_heads, key_rows, value_rows, lengths):

time: 107 us -> 104 us (0.972)
  waiting for transfers between devices: 45.3 us -> 28.2 us
  blocking collectives: 0 us -> 14.3 us
  starting transfers between devices: 36.4 us -> 42.3 us
  local copies, waits for them, and re-layouts: 4.38 us -> 0.15 us
    ppermute x29 -> x31, waiting for transfers between devices: 43.5 us -> 22.8 us  [swap(): return lax.ppermute(value, 'seq', [(i, i ^ offset) for i in range(count)])]
    all_to_all x0 -> x1, blocking collectives: none -> 14.3 us  [exchange_body(): taken = lax.all_to_all(sent, 'seq', split_axis=1, concat_axis=0, tiled=True)]
    ppermute x29 -> x31, starting transfers between devices: 29.4 us -> 39.3 us  [swap(): return lax.ppermute(value, 'seq', [(i, i ^ offset) for i in range(count)])]
    all_to_all x1 -> x0, starting transfers between devices: 7.04 us -> none  [exchange_body(): taken = lax.all_to_all(sent, 'seq', split_axis=1, concat_axis=0, tiled=True)]
    ppermute x0 -> x2, waiting for transfers between devices: none -> 5.39 us  [cross(): return lax.ppermute(value, 'groups', [(0, 1), (1, 0)])]
    ppermute x0 -> x2, starting transfers between devices: none -> 3.01 us  [cross(): return lax.ppermute(value, 'groups', [(0, 1), (1, 0)])]
    unnamed x9 -> x4, local copies, waits for them, and re-layouts: 2.71 us -> 0.01 us
    all_to_all x1 -> x0, waiting for transfers between devices: 1.8 us -> none  [exchange_body(): taken = lax.all_to_all(sent, 'seq', split_axis=1, concat_axis=0, tiled=True)]
  transfers between devices with their start and end apart: 30 -> 33, of which waited for: 17 -> 17; matrix products, arithmetic and copies ran while one was open for 2% -> 0% of each run, Pallas kernels for 10% -> 10%
where the time goes in v2:
time: 104 us
  starting transfers between devices  42.3 us (41%)
  waiting for transfers between devices  28.2 us (27%)
  Pallas kernels  18.2 us (18%)
  blocking collectives  14.3 us (14%)
    ppermute x31, starting transfers between devices, swap(): return lax.ppermute(value, 'seq', [(i, i ^ offset) for i in range(count)])  39.3 us
    ppermute x31, waiting for transfers between devices, swap(): return lax.ppermute(value, 'seq', [(i, i ^ offset) for i in range(count)])  22.8 us
    pallas_call x10, Pallas kernels, call(): pl.pallas_call(kernel, out_shape=tuple((jax.ShapeDtypeStruct(s, d) for s,...  18.2 us
    all_to_all x1, blocking collectives, exchange_body(): taken = lax.all_to_all(sent, 'seq', split_axis=1, concat_axis=0, tiled=True)  14.3 us
    ppermute x2, waiting for transfers between devices, cross(): return lax.ppermute(value, 'groups', [(0, 1), (1, 0)])  5.39 us
    ppermute x2, starting transfers between devices, cross(): return lax.ppermute(value, 'groups', [(0, 1), (1, 0)])  3.01 us
  transfers between devices with their start and end apart: 33, of which 17 were waited for; matrix products, arithmetic and copies ran while one was open for 0% of the time, Pallas kernels for 10%

profile of v2, /device:TPU:0, one launch (start us, length us, event | category | flops | bytes accessed | tf_op | source)
XLA Modules:
  0.0 104.0 jit_solution(5061678617536863147)
XLA Ops:
  2.9 14.3 %all_to_all.15 = bf16[2,16,1664]{2,0,1:T(2,128)(2,1)S(1)} all-to-all(bf16[2,16,1664]{2,0,1:T(2,128)(2,1)S(1)} %copy.16), channel_id=1, replica_groups=mesh['groups'=2,'seq'=16] {'seq'}, dimensions={1} | all-to-all | bytes 212992 | tf_op jit(solution)/shard_map/all_to_all | solution.py:446
  17.3 2.6 %shard_map.141 = (bf16[16,1024]{1,0:T(8,128)(2,1)S(1)}, bf16[16,1024]{1,0:T(8,128)(2,1)S(1)}) custom-call(s32[1]{0:T(128)} %bitcast.at_ref, bf16[32,1664]{1,0:T(8,128)(2,1)S(1)} %reshape.32.row_ref, s32[32,128]{1,0:T(8,128)S(1)} %get-tuple-element.22.length_ref, bf16[2048,128]{1,0:T(8,128)(2,1)} %bitcast.15, bf16[2048,128]{1,0:T(8,128)(2,1)} %bitcast.16), custom_call_target="tpu_custom_call" | custom-call | flops 268435456 | bytes 1048576 | tf_op jit(solution)/shard_map/pallas_call | solution.py:30
  20.9 1.6 %collective-permute-start.10 = (bf16[2,64,256]{2,1,0:T(8,128)(2,1)S(1)}, bf16[2,64,256]{2,1,0:T(8,128)(2,1)S(1)}, u32[]{:S(2)}, u32[]{:S(2)}) collective-permute-start(bf16[2,64,256]{2,1,0:T(8,128)(2,1)S(1)} %get-tuple-element.26), channel_id=1, source_target_pairs={{0,4},{1,5},{2,6},{3,7},{4,0},{5,1},{6,2},{7,3},{8,12},{9,13},{10,... | collective-permute-start | bytes 196616 | tf_op jit(solution)/shard_map/ppermute | solution.py:382
  22.6 2.6 %collective-permute-start.11 = (bf16[2,64,256]{2,1,0:T(8,128)(2,1)S(1)}, bf16[2,64,256]{2,1,0:T(8,128)(2,1)S(1)}, u32[]{:S(2)}, u32[]{:S(2)}) collective-permute-start(bf16[2,64,256]{2,1,0:T(8,128)(2,1)S(1)} %get-tuple-element.27), channel_id=1, source_target_pairs={{0,8},{1,9},{2,10},{3,11},{4,12},{5,13},{6,14},{7,15},{8,0},{9,1},... | collective-permute-start | bytes 196616 | tf_op jit(solution)/shard_map/ppermute | solution.py:382
  25.5 4.4 %collective-permute-start.12 = (bf16[2,64,256]{2,1,0:T(8,128)(2,1)S(1)}, bf16[2,64,256]{2,1,0:T(8,128)(2,1)S(1)}, u32[]{:S(2)}, u32[]{:S(2)}) collective-permute-start(bf16[2,64,256]{2,1,0:T(8,128)(2,1)S(1)} %get-tuple-element.28), channel_id=1, source_target_pairs={{0,12},{1,13},{2,14},{3,15},{4,8},{5,9},{6,10},{7,11},{8,4},{9,5},... | collective-permute-start | bytes 196616 | tf_op jit(solution)/shard_map/ppermute | solution.py:382
  29.9 2.1 %collective-permute-start.8 = (bf16[2,16,1024]{2,1,0:T(8,128)(2,1)S(1)}, bf16[2,16,1024]{2,1,0:T(8,128)(2,1)S(1)}, u32[]{:S(2)}, u32[]{:S(2)}) collective-permute-start(bf16[2,16,1024]{2,1,0:T(8,128)(2,1)S(1)} %pad_maximum_fusion.refs_4_.refs_0_), channel_id=1, source_target_pairs={{0,12},{1,13},{2,14},{3,15},{4,8},{5,9},{6,10},{7,11},{8,4},{9,5},... | collective-permute-start | bytes 196616 | tf_op jit(solution)/shard_map/ppermute | solution.py:382
  32.3 4.0 %collective-permute-start.6 = (bf16[2,16,1024]{2,1,0:T(8,128)(2,1)S(1)}, bf16[2,16,1024]{2,1,0:T(8,128)(2,1)S(1)}, u32[]{:S(2)}, u32[]{:S(2)}) collective-permute-start(bf16[2,16,1024]{2,1,0:T(8,128)(2,1)S(1)} %pad_maximum_fusion.refs_4_.refs_0_), channel_id=1, source_target_pairs={{0,8},{1,9},{2,10},{3,11},{4,12},{5,13},{6,14},{7,15},{8,0},{9,1},... | collective-permute-start | bytes 196616 | tf_op jit(solution)/shard_map/ppermute | solution.py:382
  37.0 1.8 %collective-permute-done.6.refs_4_ = bf16[2,16,1024]{2,1,0:T(8,128)(2,1)S(1)} collective-permute-done((bf16[2,16,1024]{2,1,0:T(8,128)(2,1)S(1)}, bf16[2,16,1024]{2,1,0:T(8,128)(2,1)S(1)}, u32[]{:S(2)}, u32[]{:S(2)}) %collective-permute-start.6) | collective-permute-done | bytes 65568 | tf_op jit(solution)/shard_map/ppermute | solution.py:382
  43.1 2.4 %collective-permute-done.16.refs_12_ = bf16[4,64,256]{2,1,0:T(8,128)(2,1)S(1)} collective-permute-done((bf16[4,64,256]{2,1,0:T(8,128)(2,1)S(1)}, bf16[4,64,256]{2,1,0:T(8,128)(2,1)S(1)}, u32[]{:S(2)}, u32[]{:S(2)}) %collective-permute-start.16) | collective-permute-done | bytes 131104 | tf_op jit(solution)/shard_map/ppermute | solution.py:382
  47.0 1.5 %collective-permute-start.9 = (bf16[2,16,1024]{2,1,0:T(8,128)(2,1)S(1)}, bf16[2,16,1024]{2,1,0:T(8,128)(2,1)S(1)}, u32[]{:S(2)}, u32[]{:S(2)}) collective-permute-start(bf16[2,16,1024]{2,1,0:T(8,128)(2,1)S(1)} %collective-permute-done.8.refs_6_), channel_id=1, source_target_pairs={{0,2},{1,3},{2,0},{3,1},{4,6},{5,7},{6,4},{7,5},{8,10},{9,11},{10,... | collective-permute-start | bytes 196616 | tf_op jit(solution)/shard_map/ppermute | solution.py:382
  48.5 1.9 %collective-permute-done.13.refs_9_ = bf16[4,64,256]{2,1,0:T(8,128)(2,1)S(1)} collective-permute-done((bf16[4,64,256]{2,1,0:T(8,128)(2,1)S(1)}, bf16[4,64,256]{2,1,0:T(8,128)(2,1)S(1)}, u32[]{:S(2)}, u32[]{:S(2)}) %collective-permute-start.13) | collective-permute-done | bytes 131104 | tf_op jit(solution)/shard_map/ppermute | solution.py:386
  57.8 3.5 %collective-permute-done.17.refs_13_ = bf16[4,64,256]{2,1,0:T(8,128)(2,1)S(1)} collective-permute-done((bf16[4,64,256]{2,1,0:T(8,128)(2,1)S(1)}, bf16[4,64,256]{2,1,0:T(8,128)(2,1)S(1)}, u32[]{:S(2)}, u32[]{:S(2)}) %collective-permute-start.17) | collective-permute-done | bytes 131104 | tf_op jit(solution)/shard_map/ppermute | solution.py:386
  63.2 2.4 %collective-permute-start.22 = (bf16[128,256]{1,0:T(8,128)(2,1)S(1)}, bf16[128,256]{1,0:T(8,128)(2,1)S(1)}, u32[]{:S(2)}, u32[]{:S(2)}) collective-permute-start(bf16[128,256]{1,0:T(8,128)(2,1)S(1)} %shard_map.144.refs_0_), channel_id=1, source_target_pairs={{0,12},{1,13},{2,14},{3,15},{4,8},{5,9},{6,10},{7,11},{8,4},{9,5},... | collective-permute-start | bytes 196616 | tf_op jit(solution)/shard_map/ppermute | solution.py:382
  65.6 4.2 %collective-permute-done.22.refs_3_ = bf16[128,256]{1,0:T(8,128)(2,1)S(1)} collective-permute-done((bf16[128,256]{1,0:T(8,128)(2,1)S(1)}, bf16[128,256]{1,0:T(8,128)(2,1)S(1)}, u32[]{:S(2)}, u32[]{:S(2)}) %collective-permute-start.22) | collective-permute-done | bytes 65568 | tf_op jit(solution)/shard_map/ppermute | solution.py:382
  74.1 1.6 %collective-permute-start.27 = (bf16[128,256]{1,0:T(8,128)(2,1)S(1)}, bf16[128,256]{1,0:T(8,128)(2,1)S(1)}, u32[]{:S(2)}, u32[]{:S(2)}) collective-permute-start(bf16[128,256]{1,0:T(8,128)(2,1)S(1)} %collective-permute-done.22.refs_3_), channel_id=1, source_target_pairs={{0,2},{1,3},{2,0},{3,1},{4,6},{5,7},{6,4},{7,5},{8,10},{9,11},{10,... | collective-permute-start | bytes 196616 | tf_op jit(solution)/shard_map/ppermute | solution.py:382
  76.1 1.6 %collective-permute-start.25 = (bf16[128,256]{1,0:T(8,128)(2,1)S(1)}, bf16[128,256]{1,0:T(8,128)(2,1)S(1)}, u32[]{:S(2)}, u32[]{:S(2)}) collective-permute-start(bf16[128,256]{1,0:T(8,128)(2,1)S(1)} %collective-permute-done.20.refs_1_), channel_id=1, source_target_pairs={{0,2},{1,3},{2,0},{3,1},{4,6},{5,7},{6,4},{7,5},{8,10},{9,11},{10,... | collective-permute-start | bytes 196616 | tf_op jit(solution)/shard_map/ppermute | solution.py:382
  77.8 4.8 %shard_map.145.partial_ref = f32[4,128,768]{2,1,0:T(8,128)S(1)} custom-call(s32[1]{0:T(128)} %bitcast.at_ref, bf16[1,2048]{1,0:T(2,128)(2,1)S(1)} %reshape.30.gain_ref, bf16[2,2048,384]{2,1,0:T(8,128)(2,1)S(1)} %collective-permute-done.gate_ref, bf16[2,2048,384]{2,1,0:T(8,128)(2,1)} %collective-permute-done.1.up_ref, bf16[2,2048,384]{2,1,0:T(8,128)(2,1)} %gate_hbm.3, ...), custom_call_target="tpu_custom_call" | custom-call | flops 805306368 | bytes 6291456 | tf_op jit(solution)/shard_map/pallas_call | solution.py:30
  82.7 7.4 %shard_map.146 = (bf16[16,2048]{1,0:T(8,128)(2,1)}, bf16[2,16,2048]{2,1,0:T(8,128)(2,1)S(1)}, bf16[2,16,2048]{2,1,0:T(8,128)(2,1)S(1)}, bf16[2,16,2048]{2,1,0:T(8,128)(2,1)S(1)}, bf16[2,16,2048]{2,1,0:T(8,128)(2,1)S(1)}) custom-call(s32[1]{0:T(128)} %bitcast.at_ref, bf16[1,2048]{1,0:T(2,128)(2,1)S(1)} %reshape.30.gain_ref, ...), custom_call_target="tpu_custom_call" | custom-call | flops 1610612736 | bytes 12582912 | tf_op jit(solution)/shard_map/pallas_call | solution.py:30
  90.5 1.6 %collective-permute-start.31 = (bf16[2,16,2048]{2,1,0:T(8,128)(2,1)S(1)}, bf16[2,16,2048]{2,1,0:T(8,128)(2,1)S(1)}, u32[]{:S(2)}, u32[]{:S(2)}) collective-permute-start(bf16[2,16,2048]{2,1,0:T(8,128)(2,1)S(1)} %get-tuple-element.37), channel_id=1, source_target_pairs={{0,2},{1,3},{2,0},{3,1},{4,6},{5,7},{6,4},{7,5},{8,10},{9,11},{10,... | collective-permute-start | bytes 393224 | tf_op jit(solution)/shard_map/ppermute | solution.py:382
  92.2 2.9 %collective-permute-done.28.piece_ref = bf16[2,16,2048]{2,1,0:T(8,128)(2,1)S(1)} collective-permute-done((bf16[2,16,2048]{2,1,0:T(8,128)(2,1)S(1)}, bf16[2,16,2048]{2,1,0:T(8,128)(2,1)S(1)}, u32[]{:S(2)}, u32[]{:S(2)}) %collective-permute-start.28) | collective-permute-done | bytes 131104 | tf_op jit(solution)/shard_map/ppermute | solution.py:382
  95.1 2.3 %collective-permute-start.29 = (bf16[16,2048]{1,0:T(8,128)(2,1)S(1)}, bf16[16,2048]{1,0:T(8,128)(2,1)S(1)}, u32[]{:S(2)}, u32[]{:S(2)}) collective-permute-start(bf16[16,2048]{1,0:T(8,128)(2,1)S(1)} %get-tuple-element.34), channel_id=1, source_target_pairs={{0,12},{1,13},{2,14},{3,15},{4,8},{5,9},{6,10},{7,11},{8,4},{9,5},... | collective-permute-start | bytes 196616 | tf_op jit(solution)/shard_map/ppermute | solution.py:382
  98.1 1.6 %collective-permute-start.32 = (bf16[16,2048]{1,0:T(8,128)(2,1)S(1)}, bf16[16,2048]{1,0:T(8,128)(2,1)S(1)}, u32[]{:S(2)}, u32[]{:S(2)}) collective-permute-start(bf16[16,2048]{1,0:T(8,128)(2,1)S(1)} %get-tuple-element.38), channel_id=1, source_target_pairs={{0,4},{1,5},{2,6},{3,7},{4,0},{5,1},{6,2},{7,3},{8,12},{9,13},{10,... | collective-permute-start | bytes 196616 | tf_op jit(solution)/shard_map/ppermute | solution.py:382
  99.7 1.6 %collective-permute-done.29.refs_0_ = bf16[16,2048]{1,0:T(8,128)(2,1)S(1)} collective-permute-done((bf16[16,2048]{1,0:T(8,128)(2,1)S(1)}, bf16[16,2048]{1,0:T(8,128)(2,1)S(1)}, u32[]{:S(2)}, u32[]{:S(2)}) %collective-permute-start.29) | collective-permute-done | bytes 65568 | tf_op jit(solution)/shard_map/ppermute | solution.py:382
  101.3 2.0 %collective-permute-done.30.refs_1_ = bf16[16,2048]{1,0:T(8,128)(2,1)S(1)} collective-permute-done((bf16[16,2048]{1,0:T(8,128)(2,1)S(1)}, bf16[16,2048]{1,0:T(8,128)(2,1)S(1)}, u32[]{:S(2)}, u32[]{:S(2)}) %collective-permute-start.30) | collective-permute-done | bytes 65568 | tf_op jit(solution)/shard_map/ppermute | solution.py:382
  (62 shorter events, 26.1 us)
Async XLA Ops:
  0.6 75.1 %collective-permute-start = (bf16[2,2048,384]{2,1,0:T(8,128)(2,1)}, bf16[2,2048,384]{2,1,0:T(8,128)(2,1)S(1)}, u32[]{:S(2)}, u32[]{:S(2)}) collective-permute-start(bf16[2,2048,384]{2,1,0:T(8,128)(2,1)} %gate_hbm.3), channel_id=1, source_target_pairs={{0,1},{1,0},{2,3},{3,2},{4,5},{5,4},{6,7},{7,6},{8,9},{9,8},{10,11... | collective-permute-start | bytes 9437192 | tf_op jit(solution)/shard_map/ppermute | solution.py:382
  1.2 74.9 %collective-permute-start.1 = (bf16[2,2048,384]{2,1,0:T(8,128)(2,1)}, bf16[2,2048,384]{2,1,0:T(8,128)(2,1)}, u32[]{:S(2)}, u32[]{:S(2)}) collective-permute-start(bf16[2,2048,384]{2,1,0:T(8,128)(2,1)} %up_hbm.3), channel_id=1, source_target_pairs={{0,1},{1,0},{2,3},{3,2},{4,5},{5,4},{6,7},{7,6},{8,9},{9,8},{10,11... | collective-permute-start | bytes 9437192 | tf_op jit(solution)/shard_map/ppermute | solution.py:382
  1.3 81.4 %collective-permute-start.23 = (bf16[2,384,2048]{2,1,0:T(8,128)(2,1)}, bf16[2,384,2048]{2,1,0:T(8,128)(2,1)}, u32[]{:S(2)}, u32[]{:S(2)}) collective-permute-start(bf16[2,384,2048]{2,1,0:T(8,128)(2,1)} %down_hbm.1), channel_id=1, source_target_pairs={{0,1},{1,0},{2,3},{3,2},{4,5},{5,4},{6,7},{7,6},{8,9},{9,8},{10,11... | collective-permute-start | bytes 9437192 | tf_op jit(solution)/shard_map/ppermute | solution.py:382
  20.9 4.5 %collective-permute-start.10 = (bf16[2,64,256]{2,1,0:T(8,128)(2,1)S(1)}, bf16[2,64,256]{2,1,0:T(8,128)(2,1)S(1)}, u32[]{:S(2)}, u32[]{:S(2)}) collective-permute-start(bf16[2,64,256]{2,1,0:T(8,128)(2,1)S(1)} %get-tuple-element.26), channel_id=1, source_target_pairs={{0,4},{1,5},{2,6},{3,7},{4,0},{5,1},{6,2},{7,3},{8,12},{9,13},{10,... | collective-permute-start | bytes 196616 | tf_op jit(solution)/shard_map/ppermute | solution.py:382
  22.6 7.3 %collective-permute-start.11 = (bf16[2,64,256]{2,1,0:T(8,128)(2,1)S(1)}, bf16[2,64,256]{2,1,0:T(8,128)(2,1)S(1)}, u32[]{:S(2)}, u32[]{:S(2)}) collective-permute-start(bf16[2,64,256]{2,1,0:T(8,128)(2,1)S(1)} %get-tuple-element.27), channel_id=1, source_target_pairs={{0,8},{1,9},{2,10},{3,11},{4,12},{5,13},{6,14},{7,15},{8,0},{9,1},... | collective-permute-start | bytes 196616 | tf_op jit(solution)/shard_map/ppermute | solution.py:382
  25.5 6.8 %collective-permute-start.12 = (bf16[2,64,256]{2,1,0:T(8,128)(2,1)S(1)}, bf16[2,64,256]{2,1,0:T(8,128)(2,1)S(1)}, u32[]{:S(2)}, u32[]{:S(2)}) collective-permute-start(bf16[2,64,256]{2,1,0:T(8,128)(2,1)S(1)} %get-tuple-element.28), channel_id=1, source_target_pairs={{0,12},{1,13},{2,14},{3,15},{4,8},{5,9},{6,10},{7,11},{8,4},{9,5},... | collective-permute-start | bytes 196616 | tf_op jit(solution)/shard_map/ppermute | solution.py:382
  29.9 6.3 %collective-permute-start.8 = (bf16[2,16,1024]{2,1,0:T(8,128)(2,1)S(1)}, bf16[2,16,1024]{2,1,0:T(8,128)(2,1)S(1)}, u32[]{:S(2)}, u32[]{:S(2)}) collective-permute-start(bf16[2,16,1024]{2,1,0:T(8,128)(2,1)S(1)} %pad_maximum_fusion.refs_4_.refs_0_), channel_id=1, source_target_pairs={{0,12},{1,13},{2,14},{3,15},{4,8},{5,9},{6,10},{7,11},{8,4},{9,5},... | collective-permute-start | bytes 196616 | tf_op jit(solution)/shard_map/ppermute | solution.py:382
  32.3 6.6 %collective-permute-start.6 = (bf16[2,16,1024]{2,1,0:T(8,128)(2,1)S(1)}, bf16[2,16,1024]{2,1,0:T(8,128)(2,1)S(1)}, u32[]{:S(2)}, u32[]{:S(2)}) collective-permute-start(bf16[2,16,1024]{2,1,0:T(8,128)(2,1)S(1)} %pad_maximum_fusion.refs_4_.refs_0_), channel_id=1, source_target_pairs={{0,8},{1,9},{2,10},{3,11},{4,12},{5,13},{6,14},{7,15},{8,0},{9,1},... | collective-permute-start | bytes 196616 | tf_op jit(solution)/shard_map/ppermute | solution.py:382
  40.5 5.0 %collective-permute-start.16 = (bf16[4,64,256]{2,1,0:T(8,128)(2,1)S(1)}, bf16[4,64,256]{2,1,0:T(8,128)(2,1)S(1)}, u32[]{:S(2)}, u32[]{:S(2)}) collective-permute-start(bf16[4,64,256]{2,1,0:T(8,128)(2,1)S(1)} %get-tuple-element.30), channel_id=1, source_target_pairs={{0,2},{1,3},{2,0},{3,1},{4,6},{5,7},{6,4},{7,5},{8,10},{9,11},{10,... | collective-permute-start | bytes 393224 | tf_op jit(solution)/shard_map/ppermute | solution.py:382
  45.5 5.0 %collective-permute-start.13 = (bf16[4,64,256]{2,1,0:T(8,128)(2,1)S(1)}, bf16[4,64,256]{2,1,0:T(8,128)(2,1)S(1)}, u32[]{:S(2)}, u32[]{:S(2)}) collective-permute-start(bf16[4,64,256]{2,1,0:T(8,128)(2,1)S(1)} %get-tuple-element.29.refs_8_), channel_id=1, source_target_pairs={{0,16},{16,0},{1,17},{17,1},{2,18},{18,2},{3,19},{19,3},{4,20},{20... | collective-permute-start | bytes 393224 | tf_op jit(solution)/shard_map/ppermute | solution.py:386
  47.0 5.0 %collective-permute-start.9 = (bf16[2,16,1024]{2,1,0:T(8,128)(2,1)S(1)}, bf16[2,16,1024]{2,1,0:T(8,128)(2,1)S(1)}, u32[]{:S(2)}, u32[]{:S(2)}) collective-permute-start(bf16[2,16,1024]{2,1,0:T(8,128)(2,1)S(1)} %collective-permute-done.8.refs_6_), channel_id=1, source_target_pairs={{0,2},{1,3},{2,0},{3,1},{4,6},{5,7},{6,4},{7,5},{8,10},{9,11},{10,... | collective-permute-start | bytes 196616 | tf_op jit(solution)/shard_map/ppermute | solution.py:382
  52.0 4.3 %collective-permute-start.5 = (bf16[2,16,1024]{2,1,0:T(8,128)(2,1)S(1)}, bf16[2,16,1024]{2,1,0:T(8,128)(2,1)S(1)}, u32[]{:S(2)}, u32[]{:S(2)}) collective-permute-start(bf16[2,16,1024]{2,1,0:T(8,128)(2,1)S(1)} %collective-permute-done.4.refs_2_), channel_id=1, source_target_pairs={{0,2},{1,3},{2,0},{3,1},{4,6},{5,7},{6,4},{7,5},{8,10},{9,11},{10,... | collective-permute-start | bytes 196616 | tf_op jit(solution)/shard_map/ppermute | solution.py:382
  56.3 5.0 %collective-permute-start.17 = (bf16[4,64,256]{2,1,0:T(8,128)(2,1)S(1)}, bf16[4,64,256]{2,1,0:T(8,128)(2,1)S(1)}, u32[]{:S(2)}, u32[]{:S(2)}) collective-permute-start(bf16[4,64,256]{2,1,0:T(8,128)(2,1)S(1)} %collective-permute-done.16.refs_12_), channel_id=1, source_target_pairs={{0,16},{16,0},{1,17},{17,1},{2,18},{18,2},{3,19},{19,3},{4,20},{20... | collective-permute-start | bytes 393224 | tf_op jit(solution)/shard_map/ppermute | solution.py:386
  63.2 6.7 %collective-permute-start.22 = (bf16[128,256]{1,0:T(8,128)(2,1)S(1)}, bf16[128,256]{1,0:T(8,128)(2,1)S(1)}, u32[]{:S(2)}, u32[]{:S(2)}) collective-permute-start(bf16[128,256]{1,0:T(8,128)(2,1)S(1)} %shard_map.144.refs_0_), channel_id=1, source_target_pairs={{0,12},{1,13},{2,14},{3,15},{4,8},{5,9},{6,10},{7,11},{8,4},{9,5},... | collective-permute-start | bytes 196616 | tf_op jit(solution)/shard_map/ppermute | solution.py:382
  65.6 6.6 %collective-permute-start.21 = (bf16[128,256]{1,0:T(8,128)(2,1)S(1)}, bf16[128,256]{1,0:T(8,128)(2,1)S(1)}, u32[]{:S(2)}, u32[]{:S(2)}) collective-permute-start(bf16[128,256]{1,0:T(8,128)(2,1)S(1)} %shard_map.144.refs_0_), channel_id=1, source_target_pairs={{0,8},{1,9},{2,10},{3,11},{4,12},{5,13},{6,14},{7,15},{8,0},{9,1},... | collective-permute-start | bytes 196616 | tf_op jit(solution)/shard_map/ppermute | solution.py:382
  72.2 10.4 %collective-permute-start.24 = (bf16[128,256]{1,0:T(8,128)(2,1)S(1)}, bf16[128,256]{1,0:T(8,128)(2,1)S(1)}, u32[]{:S(2)}, u32[]{:S(2)}) collective-permute-start(bf16[128,256]{1,0:T(8,128)(2,1)S(1)} %shard_map.144.refs_0_), channel_id=1, source_target_pairs={{0,2},{1,3},{2,0},{3,1},{4,6},{5,7},{6,4},{7,5},{8,10},{9,11},{10,... | collective-permute-start | bytes 196616 | tf_op jit(solution)/shard_map/ppermute | solution.py:382
  74.1 8.5 %collective-permute-start.27 = (bf16[128,256]{1,0:T(8,128)(2,1)S(1)}, bf16[128,256]{1,0:T(8,128)(2,1)S(1)}, u32[]{:S(2)}, u32[]{:S(2)}) collective-permute-start(bf16[128,256]{1,0:T(8,128)(2,1)S(1)} %collective-permute-done.22.refs_3_), channel_id=1, source_target_pairs={{0,2},{1,3},{2,0},{3,1},{4,6},{5,7},{6,4},{7,5},{8,10},{9,11},{10,... | collective-permute-start | bytes 196616 | tf_op jit(solution)/shard_map/ppermute | solution.py:382
  75.7 6.9 %collective-permute-start.26 = (bf16[128,256]{1,0:T(8,128)(2,1)S(1)}, bf16[128,256]{1,0:T(8,128)(2,1)S(1)}, u32[]{:S(2)}, u32[]{:S(2)}) collective-permute-start(bf16[128,256]{1,0:T(8,128)(2,1)S(1)} %collective-permute-done.21.refs_2_), channel_id=1, source_target_pairs={{0,2},{1,3},{2,0},{3,1},{4,6},{5,7},{6,4},{7,5},{8,10},{9,11},{10,... | collective-permute-start | bytes 196616 | tf_op jit(solution)/shard_map/ppermute | solution.py:382
  76.1 6.5 %collective-permute-start.25 = (bf16[128,256]{1,0:T(8,128)(2,1)S(1)}, bf16[128,256]{1,0:T(8,128)(2,1)S(1)}, u32[]{:S(2)}, u32[]{:S(2)}) collective-permute-start(bf16[128,256]{1,0:T(8,128)(2,1)S(1)} %collective-permute-done.20.refs_1_), channel_id=1, source_target_pairs={{0,2},{1,3},{2,0},{3,1},{4,6},{5,7},{6,4},{7,5},{8,10},{9,11},{10,... | collective-permute-start | bytes 196616 | tf_op jit(solution)/shard_map/ppermute | solution.py:382
  90.1 5.0 %collective-permute-start.28 = (bf16[2,16,2048]{2,1,0:T(8,128)(2,1)S(1)}, bf16[2,16,2048]{2,1,0:T(8,128)(2,1)S(1)}, u32[]{:S(2)}, u32[]{:S(2)}) collective-permute-start(bf16[2,16,2048]{2,1,0:T(8,128)(2,1)S(1)} %get-tuple-element.33), channel_id=1, source_target_pairs={{0,2},{1,3},{2,0},{3,1},{4,6},{5,7},{6,4},{7,5},{8,10},{9,11},{10,... | collective-permute-start | bytes 393224 | tf_op jit(solution)/shard_map/ppermute | solution.py:382
  90.5 7.6 %collective-permute-start.31 = (bf16[2,16,2048]{2,1,0:T(8,128)(2,1)S(1)}, bf16[2,16,2048]{2,1,0:T(8,128)(2,1)S(1)}, u32[]{:S(2)}, u32[]{:S(2)}) collective-permute-start(bf16[2,16,2048]{2,1,0:T(8,128)(2,1)S(1)} %get-tuple-element.37), channel_id=1, source_target_pairs={{0,2},{1,3},{2,0},{3,1},{4,6},{5,7},{6,4},{7,5},{8,10},{9,11},{10,... | collective-permute-start | bytes 393224 | tf_op jit(solution)/shard_map/ppermute | solution.py:382
  95.1 6.1 %collective-permute-start.29 = (bf16[16,2048]{1,0:T(8,128)(2,1)S(1)}, bf16[16,2048]{1,0:T(8,128)(2,1)S(1)}, u32[]{:S(2)}, u32[]{:S(2)}) collective-permute-start(bf16[16,2048]{1,0:T(8,128)(2,1)S(1)} %get-tuple-element.34), channel_id=1, source_target_pairs={{0,12},{1,13},{2,14},{3,15},{4,8},{5,9},{6,10},{7,11},{8,4},{9,5},... | collective-permute-start | bytes 196616 | tf_op jit(solution)/shard_map/ppermute | solution.py:382
  97.4 5.9 %collective-permute-start.30 = (bf16[16,2048]{1,0:T(8,128)(2,1)S(1)}, bf16[16,2048]{1,0:T(8,128)(2,1)S(1)}, u32[]{:S(2)}, u32[]{:S(2)}) collective-permute-start(bf16[16,2048]{1,0:T(8,128)(2,1)S(1)} %get-tuple-element.35), channel_id=1, source_target_pairs={{0,8},{1,9},{2,10},{3,11},{4,12},{5,13},{6,14},{7,15},{8,0},{9,1},... | collective-permute-start | bytes 196616 | tf_op jit(solution)/shard_map/ppermute | solution.py:382
  98.1 5.2 %collective-permute-start.32 = (bf16[16,2048]{1,0:T(8,128)(2,1)S(1)}, bf16[16,2048]{1,0:T(8,128)(2,1)S(1)}, u32[]{:S(2)}, u32[]{:S(2)}) collective-permute-start(bf16[16,2048]{1,0:T(8,128)(2,1)S(1)} %get-tuple-element.38), channel_id=1, source_target_pairs={{0,4},{1,5},{2,6},{3,7},{4,0},{5,1},{6,2},{7,3},{8,12},{9,13},{10,... | collective-permute-start | bytes 196616 | tf_op jit(solution)/shard_map/ppermute | solution.py:382
  (11 other events, 113.5 us)

commit v3 on v2

--- a/solution.py
+++ b/solution.py
@@ -234,18 +234,17 @@
     ).astype(jnp.bfloat16)
 
 
-def weigh(chip, odd, pieces, gain_ref, there, own_hbm, own_ref, sems):
+def stage_kernel(*refs):
+    count = (len(refs) - 1) // 2
+    for copy in fetch(refs[:count], refs[count:-1], refs[-1]):
+        copy.wait()
+
+
+def weigh(chip, odd, pieces, gain_ref, *pairs):
     lanes = pieces[0].shape[1]
-    experts = own_ref.shape[1]
     starts = [
         pl.multiple_of((chip ^ (2 * i + odd)) * lanes, lanes) for i in range(len(pieces))
     ]
-    sources, targets = [], []
-    for i, start in enumerate(starts):
-        for m, source in enumerate(own_hbm):
-            sources.append(source.at[:, pl.ds(start, lanes), :])
-            targets.append(own_ref.at[m, :, pl.ds(i * lanes, lanes), :])
-    copies = fetch(sources, targets, sems)
     rows = jnp.concatenate(
         [
             (
@@ -257,32 +256,24 @@
         axis=1,
     )
 
-    def products(pick):
-        return [
-            jnp.dot(
-                rows,
-                jnp.concatenate([pick(0, e), pick(1, e)], axis=1),
-                preferred_element_type=jnp.float32,
-            )
-            for e in range(experts)
-        ]
-
-    out = products(
-        lambda m, e: jnp.concatenate(
-            [there[m][e, pl.ds(start, lanes), :] for start in starts], axis=0
+    def part(ref, e):
+        return jnp.concatenate([ref[e, pl.ds(start, lanes), :] for start in starts], axis=0)
+
+    return [
+        jnp.dot(
+            rows,
+            jnp.concatenate([part(gate, e), part(up, e)], axis=1),
+            preferred_element_type=jnp.float32,
         )
-    )
-    for copy in copies:
-        copy.wait()
-    return out + products(lambda m, e: own_ref[m, e])
-
-
-def gate_kernel(at_ref, gain_ref, gate_ref, up_ref, gate_hbm, up_hbm, *refs):
-    pieces, (out_ref, own_ref, sems) = refs[:-3], refs[-3:]
-    out = weigh(
-        at_ref[0] // 2, 0, pieces, gain_ref, (gate_ref, up_ref), (gate_hbm, up_hbm), own_ref, sems
-    )
-    for i, value in enumerate(out):
+        for gate, up in pairs
+        for e in range(gate.shape[0])
+    ]
+
+
+def gate_kernel(at_ref, gain_ref, gate_ref, up_ref, gate_own_ref, up_own_ref, *refs):
+    pieces, out_ref = refs[:-1], refs[-1]
+    pairs = ((gate_ref, up_ref), (gate_own_ref, up_own_ref))
+    for i, value in enumerate(weigh(at_ref[0] // 2, 0, pieces, gain_ref, *pairs)):
         out_ref[i] = value
 
 
@@ -298,8 +289,8 @@
     gain_ref,
     gate_ref,
     up_ref,
-    gate_hbm,
-    up_hbm,
+    gate_own_ref,
+    up_own_ref,
     partial_ref,
     info_ref,
     down_ref,
@@ -307,7 +298,7 @@
     *refs,
 ):
     near, far, projected_ref = refs[: chips // 2], refs[chips // 2 : chips], refs[chips]
-    outs, (result_ref, own_ref, sems) = refs[chips + 1 : -3], refs[-3:]
+    outs, result_ref = refs[chips + 1 : -1], refs[-1]
     me = at_ref[0]
     chip, core = me // 2, me % 2
     rows, lanes = near[0].shape
@@ -335,9 +326,8 @@
     share = jnp.where(mine, info[:, width : 2 * width] + info[:, 2 * width :], 0.0)
     whole = jnp.sum(share, axis=1, keepdims=True)
 
-    out = weigh(
-        chip, 1, far, gain_ref, (gate_ref, up_ref), (gate_hbm, up_hbm), own_ref, sems
-    )
+    pairs = ((gate_ref, up_ref), (gate_own_ref, up_own_ref))
+    out = weigh(chip, 1, far, gain_ref, *pairs)
     hidden = []
     for d in range(2 * experts):
         device = me ^ (1 - d // experts)
@@ -486,6 +476,14 @@
     )
     beyond = swap(across, 2)
     columns_there = cross(columns)
+    own_up, = call(
+        stage_kernel,
+        [(w_up.shape, bf16)],
+        (w_up,),
+        scratch=[pltpu.SemaphoreType.DMA((1,))],
+        far=range(1),
+        vmem_mib=4,
+    )
     beyond_there = cross(beyond)
     blocks = [columns, columns_there]
     blocks += [swap(block, 1) for block in blocks]
@@ -503,14 +501,11 @@
     near, far = gather_rows(projected)
     gain = norm_gain.reshape(1, D)
     experts, _, hidden = w_gate.shape
-    own_rows = pltpu.VMEM((2, experts, D // 2, hidden), bf16)
     (partial,) = call(
         gate_kernel,
         [((2 * experts, half, 2 * hidden), jnp.float32)],
-        (at, gain, gate_peer, up_peer, w_gate, w_up, *near),
-        scratch=[own_rows, pltpu.SemaphoreType.DMA((chips,))],
-        far=(4, 5),
-        vmem_mib=16,
+        (at, gain, gate_peer, up_peer, w_gate, own_up, *near),
+        vmem_mib=10,
         flops=4 * half * w_gate.size,
         moved=4 * w_gate.size,
     )
@@ -523,7 +518,7 @@
             gate_peer,
             up_peer,
             w_gate,
-            w_up,
+            own_up,
             partial,
             taken[:, wide + 2 * HD :],
             down_peer,
@@ -531,13 +526,8 @@
             *near,
             *far,
         ),
-        scratch=[
-            pltpu.VMEM((half, D), bf16),
-            own_rows,
-            pltpu.SemaphoreType.DMA((chips,)),
-        ],
-        far=(4, 5),
-        vmem_mib=24,
+        scratch=[pltpu.VMEM((half, D), bf16)],
+        vmem_mib=14,
         flops=8 * half * w_gate.size,
         moved=8 * w_gate.size,
     )
@@ -590,7 +580,7 @@
     expert_ids,
     route_weights,
     w_gate,
-    w_up,
+    own_up,
     w_down,
 ):
     slot_count = lax.axis_size("seq")
@@ -647,7 +637,7 @@
     incoming = lax.all_to_all(outgoing, "seq", split_axis=1, concat_axis=1, tiled=True)
     row_block = incoming.reshape(exp_dev, slot_count * CAP, D)
     gate_out = jnp.einsum("ecd,edf->ecf", row_block, w_gate, preferred_element_type=jnp.float32)
-    up_out = jnp.einsum("ecd,edf->ecf", row_block, w_up, preferred_element_type=jnp.float32)
+    up_out = jnp.einsum("ecd,edf->ecf", row_block, own_up, preferred_element_type=jnp.float32)
     hidden_act = (jax.nn.silu(gate_out) * up_out).astype(jnp.bfloat16)
     expert_out = jnp.einsum(
         "ecf,efd->ecd", hidden_act, w_down, preferred_element_type=jnp.float32

time: 104 us -> 101 us (0.971)
  Pallas kernels: 18.2 us -> 16.3 us
  waiting for transfers between devices: 28.2 us -> 27.1 us
    pallas_call x10 -> x11, Pallas kernels: 18.2 us -> 16.3 us  [call(): pl.pallas_call(kernel, out_shape=tuple((jax.ShapeDtypeStruct(s, d) for s,...]
    ppermute x31, waiting for transfers between devices: 22.8 us -> 21.6 us  [swap(): return lax.ppermute(value, 'seq', [(i, i ^ offset) for i in range(count)])]
  transfers between devices with their start and end apart: 33 -> 33, of which waited for: 17 -> 15; matrix products, arithmetic and copies ran while one was open for 0% -> 0% of each run, Pallas kernels for 10% -> 10%
where the time goes in v3:
time: 101 us
  starting transfers between devices  42 us (42%)
  waiting for transfers between devices  27.1 us (27%)
  Pallas kernels  16.3 us (16%)
  blocking collectives  14.3 us (14%)
    ppermute x31, starting transfers between devices, swap(): return lax.ppermute(value, 'seq', [(i, i ^ offset) for i in range(count)])  39.1 us
    ppermute x31, waiting for transfers between devices, swap(): return lax.ppermute(value, 'seq', [(i, i ^ offset) for i in range(count)])  21.6 us
    pallas_call x11, Pallas kernels, call(): pl.pallas_call(kernel, out_shape=tuple((jax.ShapeDtypeStruct(s, d) for s,...  16.3 us
    all_to_all x1, blocking collectives, exchange_body(): taken = lax.all_to_all(sent, 'seq', split_axis=1, concat_axis=0, tiled=True)  14.3 us
    ppermute x2, waiting for transfers between devices, cross(): return lax.ppermute(value, 'groups', [(0, 1), (1, 0)])  5.44 us
    ppermute x2, starting transfers between devices, cross(): return lax.ppermute(value, 'groups', [(0, 1), (1, 0)])  2.96 us
  transfers between devices with their start and end apart: 33, of which 15 were waited for; matrix products, arithmetic and copies ran while one was open for 0% of the time, Pallas kernels for 10%

profile of v3, /device:TPU:0, one launch (start us, length us, event | category | flops | bytes accessed | tf_op | source)
XLA Modules:
  0.0 100.7 jit_solution(10040480018535817029)
XLA Ops:
  2.9 14.3 %all_to_all.15 = bf16[2,16,1664]{2,0,1:T(2,128)(2,1)S(1)} all-to-all(bf16[2,16,1664]{2,0,1:T(2,128)(2,1)S(1)} %copy.16), channel_id=1, replica_groups=mesh['groups'=2,'seq'=16] {'seq'}, dimensions={1} | all-to-all | bytes 212992 | tf_op jit(solution)/shard_map/all_to_all | solution.py:436
  17.3 2.6 %shard_map.142 = (bf16[16,1024]{1,0:T(8,128)(2,1)S(1)}, bf16[16,1024]{1,0:T(8,128)(2,1)S(1)}) custom-call(s32[1]{0:T(128)} %bitcast.at_ref, bf16[32,1664]{1,0:T(8,128)(2,1)S(1)} %reshape.32.row_ref, s32[32,128]{1,0:T(8,128)S(1)} %get-tuple-element.22.length_ref, bf16[2048,128]{1,0:T(8,128)(2,1)} %bitcast.15, bf16[2048,128]{1,0:T(8,128)(2,1)} %bitcast.16), custom_call_target="tpu_custom_call" | custom-call | flops 268435456 | bytes 1048576 | tf_op jit(solution)/shard_map/pallas_call | solution.py:30
  20.9 1.6 %collective-permute-start.10 = (bf16[2,64,256]{2,1,0:T(8,128)(2,1)S(1)}, bf16[2,64,256]{2,1,0:T(8,128)(2,1)S(1)}, u32[]{:S(2)}, u32[]{:S(2)}) collective-permute-start(bf16[2,64,256]{2,1,0:T(8,128)(2,1)S(1)} %get-tuple-element.26), channel_id=1, source_target_pairs={{0,4},{1,5},{2,6},{3,7},{4,0},{5,1},{6,2},{7,3},{8,12},{9,13},{10,... | collective-permute-start | bytes 196616 | tf_op jit(solution)/shard_map/ppermute | solution.py:372
  22.6 2.6 %collective-permute-start.11 = (bf16[2,64,256]{2,1,0:T(8,128)(2,1)S(1)}, bf16[2,64,256]{2,1,0:T(8,128)(2,1)S(1)}, u32[]{:S(2)}, u32[]{:S(2)}) collective-permute-start(bf16[2,64,256]{2,1,0:T(8,128)(2,1)S(1)} %get-tuple-element.27), channel_id=1, source_target_pairs={{0,8},{1,9},{2,10},{3,11},{4,12},{5,13},{6,14},{7,15},{8,0},{9,1},... | collective-permute-start | bytes 196616 | tf_op jit(solution)/shard_map/ppermute | solution.py:372
  25.5 4.4 %collective-permute-start.12 = (bf16[2,64,256]{2,1,0:T(8,128)(2,1)S(1)}, bf16[2,64,256]{2,1,0:T(8,128)(2,1)S(1)}, u32[]{:S(2)}, u32[]{:S(2)}) collective-permute-start(bf16[2,64,256]{2,1,0:T(8,128)(2,1)S(1)} %get-tuple-element.28), channel_id=1, source_target_pairs={{0,12},{1,13},{2,14},{3,15},{4,8},{5,9},{6,10},{7,11},{8,4},{9,5},... | collective-permute-start | bytes 196616 | tf_op jit(solution)/shard_map/ppermute | solution.py:372
  29.9 2.1 %collective-permute-start.8 = (bf16[2,16,1024]{2,1,0:T(8,128)(2,1)S(1)}, bf16[2,16,1024]{2,1,0:T(8,128)(2,1)S(1)}, u32[]{:S(2)}, u32[]{:S(2)}) collective-permute-start(bf16[2,16,1024]{2,1,0:T(8,128)(2,1)S(1)} %pad_maximum_fusion.refs_4_.refs_0_), channel_id=1, source_target_pairs={{0,12},{1,13},{2,14},{3,15},{4,8},{5,9},{6,10},{7,11},{8,4},{9,5},... | collective-permute-start | bytes 196616 | tf_op jit(solution)/shard_map/ppermute | solution.py:372
  32.3 4.0 %collective-permute-start.6 = (bf16[2,16,1024]{2,1,0:T(8,128)(2,1)S(1)}, bf16[2,16,1024]{2,1,0:T(8,128)(2,1)S(1)}, u32[]{:S(2)}, u32[]{:S(2)}) collective-permute-start(bf16[2,16,1024]{2,1,0:T(8,128)(2,1)S(1)} %pad_maximum_fusion.refs_4_.refs_0_), channel_id=1, source_target_pairs={{0,8},{1,9},{2,10},{3,11},{4,12},{5,13},{6,14},{7,15},{8,0},{9,1},... | collective-permute-start | bytes 196616 | tf_op jit(solution)/shard_map/ppermute | solution.py:372
  37.0 1.9 %collective-permute-done.6.refs_4_ = bf16[2,16,1024]{2,1,0:T(8,128)(2,1)S(1)} collective-permute-done((bf16[2,16,1024]{2,1,0:T(8,128)(2,1)S(1)}, bf16[2,16,1024]{2,1,0:T(8,128)(2,1)S(1)}, u32[]{:S(2)}, u32[]{:S(2)}) %collective-permute-start.6) | collective-permute-done | bytes 65568 | tf_op jit(solution)/shard_map/ppermute | solution.py:372
  40.5 1.5 %collective-permute-start.16 = (bf16[4,64,256]{2,1,0:T(8,128)(2,1)S(1)}, bf16[4,64,256]{2,1,0:T(8,128)(2,1)S(1)}, u32[]{:S(2)}, u32[]{:S(2)}) collective-permute-start(bf16[4,64,256]{2,1,0:T(8,128)(2,1)S(1)} %get-tuple-element.30), channel_id=1, source_target_pairs={{0,2},{1,3},{2,0},{3,1},{4,6},{5,7},{6,4},{7,5},{8,10},{9,11},{10,... | collective-permute-start | bytes 393224 | tf_op jit(solution)/shard_map/ppermute | solution.py:372
  43.1 2.4 %collective-permute-done.16.refs_12_ = bf16[4,64,256]{2,1,0:T(8,128)(2,1)S(1)} collective-permute-done((bf16[4,64,256]{2,1,0:T(8,128)(2,1)S(1)}, bf16[4,64,256]{2,1,0:T(8,128)(2,1)S(1)}, u32[]{:S(2)}, u32[]{:S(2)}) %collective-permute-start.16) | collective-permute-done | bytes 131104 | tf_op jit(solution)/shard_map/ppermute | solution.py:372
  47.0 1.5 %collective-permute-start.9 = (bf16[2,16,1024]{2,1,0:T(8,128)(2,1)S(1)}, bf16[2,16,1024]{2,1,0:T(8,128)(2,1)S(1)}, u32[]{:S(2)}, u32[]{:S(2)}) collective-permute-start(bf16[2,16,1024]{2,1,0:T(8,128)(2,1)S(1)} %collective-permute-done.8.refs_6_), channel_id=1, source_target_pairs={{0,2},{1,3},{2,0},{3,1},{4,6},{5,7},{6,4},{7,5},{8,10},{9,11},{10,... | collective-permute-start | bytes 196616 | tf_op jit(solution)/shard_map/ppermute | solution.py:372
  48.5 2.0 %collective-permute-done.13.refs_9_ = bf16[4,64,256]{2,1,0:T(8,128)(2,1)S(1)} collective-permute-done((bf16[4,64,256]{2,1,0:T(8,128)(2,1)S(1)}, bf16[4,64,256]{2,1,0:T(8,128)(2,1)S(1)}, u32[]{:S(2)}, u32[]{:S(2)}) %collective-permute-start.13) | collective-permute-done | bytes 131104 | tf_op jit(solution)/shard_map/ppermute | solution.py:376
  54.8 1.5 %collective-permute-done.5.refs_3_ = bf16[2,16,1024]{2,1,0:T(8,128)(2,1)S(1)} collective-permute-done((bf16[2,16,1024]{2,1,0:T(8,128)(2,1)S(1)}, bf16[2,16,1024]{2,1,0:T(8,128)(2,1)S(1)}, u32[]{:S(2)}, u32[]{:S(2)}) %collective-permute-start.5) | collective-permute-done | bytes 65568 | tf_op jit(solution)/shard_map/ppermute | solution.py:372
  57.8 3.5 %collective-permute-done.17.refs_13_ = bf16[4,64,256]{2,1,0:T(8,128)(2,1)S(1)} collective-permute-done((bf16[4,64,256]{2,1,0:T(8,128)(2,1)S(1)}, bf16[4,64,256]{2,1,0:T(8,128)(2,1)S(1)}, u32[]{:S(2)}, u32[]{:S(2)}) %collective-permute-start.17) | collective-permute-done | bytes 131104 | tf_op jit(solution)/shard_map/ppermute | solution.py:376
  63.2 2.4 %collective-permute-start.22 = (bf16[128,256]{1,0:T(8,128)(2,1)S(1)}, bf16[128,256]{1,0:T(8,128)(2,1)S(1)}, u32[]{:S(2)}, u32[]{:S(2)}) collective-permute-start(bf16[128,256]{1,0:T(8,128)(2,1)S(1)} %shard_map.145.refs_0_), channel_id=1, source_target_pairs={{0,12},{1,13},{2,14},{3,15},{4,8},{5,9},{6,10},{7,11},{8,4},{9,5},... | collective-permute-start | bytes 196616 | tf_op jit(solution)/shard_map/ppermute | solution.py:372
  65.6 4.3 %collective-permute-done.22.refs_3_ = bf16[128,256]{1,0:T(8,128)(2,1)S(1)} collective-permute-done((bf16[128,256]{1,0:T(8,128)(2,1)S(1)}, bf16[128,256]{1,0:T(8,128)(2,1)S(1)}, u32[]{:S(2)}, u32[]{:S(2)}) %collective-permute-start.22) | collective-permute-done | bytes 65568 | tf_op jit(solution)/shard_map/ppermute | solution.py:372
  71.0 1.9 %shard_map.140.up_own_ref = bf16[2,2048,384]{2,1,0:T(8,128)(2,1)S(1)} custom-call(bf16[2,2048,384]{2,1,0:T(8,128)(2,1)} %refs_0_.1), custom_call_target="tpu_custom_call" | custom-call | tf_op jit(solution)/shard_map/pallas_call | solution.py:30
  77.8 2.9 %shard_map.146.partial_ref = f32[4,128,768]{2,1,0:T(8,128)S(1)} custom-call(s32[1]{0:T(128)} %bitcast.at_ref, bf16[1,2048]{1,0:T(2,128)(2,1)S(1)} %reshape.30.gain_ref, bf16[2,2048,384]{2,1,0:T(8,128)(2,1)} %collective-permute-done.gate_ref, bf16[2,2048,384]{2,1,0:T(8,128)(2,1)S(1)} %collective-permute-done.1.up_ref, bf16[2,2048,384]{2,1,0:T(8,128)(2,1)S(1)} %copy-done, ...), custom_call_target="tpu_custom_call" | custom-call | flops 805306368 | bytes 6291456 | tf_op jit(solution)/shard_map/pallas_call | solution.py:30
  80.7 5.5 %shard_map.147 = (bf16[16,2048]{1,0:T(8,128)(2,1)}, bf16[2,16,2048]{2,1,0:T(8,128)(2,1)S(1)}, bf16[2,16,2048]{2,1,0:T(8,128)(2,1)S(1)}, bf16[2,16,2048]{2,1,0:T(8,128)(2,1)S(1)}, bf16[2,16,2048]{2,1,0:T(8,128)(2,1)S(1)}) custom-call(s32[1]{0:T(128)} %bitcast.at_ref, bf16[1,2048]{1,0:T(2,128)(2,1)S(1)} %reshape.30.gain_ref, ...), custom_call_target="tpu_custom_call" | custom-call | flops 1610612736 | bytes 12582912 | tf_op jit(solution)/shard_map/pallas_call | solution.py:30
  88.3 3.4 %collective-permute-done.28.piece_ref = bf16[2,16,2048]{2,1,0:T(8,128)(2,1)S(1)} collective-permute-done((bf16[2,16,2048]{2,1,0:T(8,128)(2,1)S(1)}, bf16[2,16,2048]{2,1,0:T(8,128)(2,1)S(1)}, u32[]{:S(2)}, u32[]{:S(2)}) %collective-permute-start.28) | collective-permute-done | bytes 131104 | tf_op jit(solution)/shard_map/ppermute | solution.py:372
  91.7 3.0 %collective-permute-start.29 = (bf16[16,2048]{1,0:T(8,128)(2,1)S(1)}, bf16[16,2048]{1,0:T(8,128)(2,1)S(1)}, u32[]{:S(2)}, u32[]{:S(2)}) collective-permute-start(bf16[16,2048]{1,0:T(8,128)(2,1)S(1)} %get-tuple-element.34), channel_id=1, source_target_pairs={{0,12},{1,13},{2,14},{3,15},{4,8},{5,9},{6,10},{7,11},{8,4},{9,5},... | collective-permute-start | bytes 196616 | tf_op jit(solution)/shard_map/ppermute | solution.py:372
  94.7 1.6 %collective-permute-start.32 = (bf16[16,2048]{1,0:T(8,128)(2,1)S(1)}, bf16[16,2048]{1,0:T(8,128)(2,1)S(1)}, u32[]{:S(2)}, u32[]{:S(2)}) collective-permute-start(bf16[16,2048]{1,0:T(8,128)(2,1)S(1)} %get-tuple-element.38), channel_id=1, source_target_pairs={{0,4},{1,5},{2,6},{3,7},{4,0},{5,1},{6,2},{7,3},{8,12},{9,13},{10,... | collective-permute-start | bytes 196616 | tf_op jit(solution)/shard_map/ppermute | solution.py:372
  96.2 1.6 %collective-permute-done.29.refs_0_ = bf16[16,2048]{1,0:T(8,128)(2,1)S(1)} collective-permute-done((bf16[16,2048]{1,0:T(8,128)(2,1)S(1)}, bf16[16,2048]{1,0:T(8,128)(2,1)S(1)}, u32[]{:S(2)}, u32[]{:S(2)}) %collective-permute-start.29) | collective-permute-done | bytes 65568 | tf_op jit(solution)/shard_map/ppermute | solution.py:372
  97.8 2.2 %collective-permute-done.30.refs_1_ = bf16[16,2048]{1,0:T(8,128)(2,1)S(1)} collective-permute-done((bf16[16,2048]{1,0:T(8,128)(2,1)S(1)}, bf16[16,2048]{1,0:T(8,128)(2,1)S(1)}, u32[]{:S(2)}, u32[]{:S(2)}) %collective-permute-start.30) | collective-permute-done | bytes 65568 | tf_op jit(solution)/shard_map/ppermute | solution.py:372
  (65 shorter events, 25.3 us)
Async XLA Ops:
  0.6 75.1 %collective-permute-start.1 = (bf16[2,2048,384]{2,1,0:T(8,128)(2,1)}, bf16[2,2048,384]{2,1,0:T(8,128)(2,1)S(1)}, u32[]{:S(2)}, u32[]{:S(2)}) collective-permute-start(bf16[2,2048,384]{2,1,0:T(8,128)(2,1)} %refs_0_.1), channel_id=1, source_target_pairs={{0,1},{1,0},{2,3},{3,2},{4,5},{5,4},{6,7},{7,6},{8,9},{9,8},{10,11... | collective-permute-start | bytes 9437192 | tf_op jit(solution)/shard_map/ppermute | solution.py:372
  1.2 75.2 %collective-permute-start = (bf16[2,2048,384]{2,1,0:T(8,128)(2,1)}, bf16[2,2048,384]{2,1,0:T(8,128)(2,1)}, u32[]{:S(2)}, u32[]{:S(2)}) collective-permute-start(bf16[2,2048,384]{2,1,0:T(8,128)(2,1)} %gate_own_ref.3), channel_id=1, source_target_pairs={{0,1},{1,0},{2,3},{3,2},{4,5},{5,4},{6,7},{7,6},{8,9},{9,8},{10,11... | collective-permute-start | bytes 9437192 | tf_op jit(solution)/shard_map/ppermute | solution.py:372
  1.3 79.5 %collective-permute-start.23 = (bf16[2,384,2048]{2,1,0:T(8,128)(2,1)}, bf16[2,384,2048]{2,1,0:T(8,128)(2,1)}, u32[]{:S(2)}, u32[]{:S(2)}) collective-permute-start(bf16[2,384,2048]{2,1,0:T(8,128)(2,1)} %down_hbm.1), channel_id=1, source_target_pairs={{0,1},{1,0},{2,3},{3,2},{4,5},{5,4},{6,7},{7,6},{8,9},{9,8},{10,11... | collective-permute-start | bytes 9437192 | tf_op jit(solution)/shard_map/ppermute | solution.py:372
  20.9 4.5 %collective-permute-start.10 = (bf16[2,64,256]{2,1,0:T(8,128)(2,1)S(1)}, bf16[2,64,256]{2,1,0:T(8,128)(2,1)S(1)}, u32[]{:S(2)}, u32[]{:S(2)}) collective-permute-start(bf16[2,64,256]{2,1,0:T(8,128)(2,1)S(1)} %get-tuple-element.26), channel_id=1, source_target_pairs={{0,4},{1,5},{2,6},{3,7},{4,0},{5,1},{6,2},{7,3},{8,12},{9,13},{10,... | collective-permute-start | bytes 196616 | tf_op jit(solution)/shard_map/ppermute | solution.py:372
  22.6 7.3 %collective-permute-start.11 = (bf16[2,64,256]{2,1,0:T(8,128)(2,1)S(1)}, bf16[2,64,256]{2,1,0:T(8,128)(2,1)S(1)}, u32[]{:S(2)}, u32[]{:S(2)}) collective-permute-start(bf16[2,64,256]{2,1,0:T(8,128)(2,1)S(1)} %get-tuple-element.27), channel_id=1, source_target_pairs={{0,8},{1,9},{2,10},{3,11},{4,12},{5,13},{6,14},{7,15},{8,0},{9,1},... | collective-permute-start | bytes 196616 | tf_op jit(solution)/shard_map/ppermute | solution.py:372
  25.5 6.8 %collective-permute-start.12 = (bf16[2,64,256]{2,1,0:T(8,128)(2,1)S(1)}, bf16[2,64,256]{2,1,0:T(8,128)(2,1)S(1)}, u32[]{:S(2)}, u32[]{:S(2)}) collective-permute-start(bf16[2,64,256]{2,1,0:T(8,128)(2,1)S(1)} %get-tuple-element.28), channel_id=1, source_target_pairs={{0,12},{1,13},{2,14},{3,15},{4,8},{5,9},{6,10},{7,11},{8,4},{9,5},... | collective-permute-start | bytes 196616 | tf_op jit(solution)/shard_map/ppermute | solution.py:372
  29.9 6.4 %collective-permute-start.8 = (bf16[2,16,1024]{2,1,0:T(8,128)(2,1)S(1)}, bf16[2,16,1024]{2,1,0:T(8,128)(2,1)S(1)}, u32[]{:S(2)}, u32[]{:S(2)}) collective-permute-start(bf16[2,16,1024]{2,1,0:T(8,128)(2,1)S(1)} %pad_maximum_fusion.refs_4_.refs_0_), channel_id=1, source_target_pairs={{0,12},{1,13},{2,14},{3,15},{4,8},{5,9},{6,10},{7,11},{8,4},{9,5},... | collective-permute-start | bytes 196616 | tf_op jit(solution)/shard_map/ppermute | solution.py:372
  32.3 6.6 %collective-permute-start.6 = (bf16[2,16,1024]{2,1,0:T(8,128)(2,1)S(1)}, bf16[2,16,1024]{2,1,0:T(8,128)(2,1)S(1)}, u32[]{:S(2)}, u32[]{:S(2)}) collective-permute-start(bf16[2,16,1024]{2,1,0:T(8,128)(2,1)S(1)} %pad_maximum_fusion.refs_4_.refs_0_), channel_id=1, source_target_pairs={{0,8},{1,9},{2,10},{3,11},{4,12},{5,13},{6,14},{7,15},{8,0},{9,1},... | collective-permute-start | bytes 196616 | tf_op jit(solution)/shard_map/ppermute | solution.py:372
  40.5 5.0 %collective-permute-start.16 = (bf16[4,64,256]{2,1,0:T(8,128)(2,1)S(1)}, bf16[4,64,256]{2,1,0:T(8,128)(2,1)S(1)}, u32[]{:S(2)}, u32[]{:S(2)}) collective-permute-start(bf16[4,64,256]{2,1,0:T(8,128)(2,1)S(1)} %get-tuple-element.30), channel_id=1, source_target_pairs={{0,2},{1,3},{2,0},{3,1},{4,6},{5,7},{6,4},{7,5},{8,10},{9,11},{10,... | collective-permute-start | bytes 393224 | tf_op jit(solution)/shard_map/ppermute | solution.py:372
  45.5 5.0 %collective-permute-start.13 = (bf16[4,64,256]{2,1,0:T(8,128)(2,1)S(1)}, bf16[4,64,256]{2,1,0:T(8,128)(2,1)S(1)}, u32[]{:S(2)}, u32[]{:S(2)}) collective-permute-start(bf16[4,64,256]{2,1,0:T(8,128)(2,1)S(1)} %get-tuple-element.29.refs_8_), channel_id=1, source_target_pairs={{0,16},{16,0},{1,17},{17,1},{2,18},{18,2},{3,19},{19,3},{4,20},{20... | collective-permute-start | bytes 393224 | tf_op jit(solution)/shard_map/ppermute | solution.py:376
  47.0 5.0 %collective-permute-start.9 = (bf16[2,16,1024]{2,1,0:T(8,128)(2,1)S(1)}, bf16[2,16,1024]{2,1,0:T(8,128)(2,1)S(1)}, u32[]{:S(2)}, u32[]{:S(2)}) collective-permute-start(bf16[2,16,1024]{2,1,0:T(8,128)(2,1)S(1)} %collective-permute-done.8.refs_6_), channel_id=1, source_target_pairs={{0,2},{1,3},{2,0},{3,1},{4,6},{5,7},{6,4},{7,5},{8,10},{9,11},{10,... | collective-permute-start | bytes 196616 | tf_op jit(solution)/shard_map/ppermute | solution.py:372
  56.3 5.0 %collective-permute-start.17 = (bf16[4,64,256]{2,1,0:T(8,128)(2,1)S(1)}, bf16[4,64,256]{2,1,0:T(8,128)(2,1)S(1)}, u32[]{:S(2)}, u32[]{:S(2)}) collective-permute-start(bf16[4,64,256]{2,1,0:T(8,128)(2,1)S(1)} %collective-permute-done.16.refs_12_), channel_id=1, source_target_pairs={{0,16},{16,0},{1,17},{17,1},{2,18},{18,2},{3,19},{19,3},{4,20},{20... | collective-permute-start | bytes 393224 | tf_op jit(solution)/shard_map/ppermute | solution.py:376
  63.2 6.7 %collective-permute-start.22 = (bf16[128,256]{1,0:T(8,128)(2,1)S(1)}, bf16[128,256]{1,0:T(8,128)(2,1)S(1)}, u32[]{:S(2)}, u32[]{:S(2)}) collective-permute-start(bf16[128,256]{1,0:T(8,128)(2,1)S(1)} %shard_map.145.refs_0_), channel_id=1, source_target_pairs={{0,12},{1,13},{2,14},{3,15},{4,8},{5,9},{6,10},{7,11},{8,4},{9,5},... | collective-permute-start | bytes 196616 | tf_op jit(solution)/shard_map/ppermute | solution.py:372
  65.5 7.4 %collective-permute-start.21 = (bf16[128,256]{1,0:T(8,128)(2,1)S(1)}, bf16[128,256]{1,0:T(8,128)(2,1)S(1)}, u32[]{:S(2)}, u32[]{:S(2)}) collective-permute-start(bf16[128,256]{1,0:T(8,128)(2,1)S(1)} %shard_map.145.refs_0_), channel_id=1, source_target_pairs={{0,8},{1,9},{2,10},{3,11},{4,12},{5,13},{6,14},{7,15},{8,0},{9,1},... | collective-permute-start | bytes 196616 | tf_op jit(solution)/shard_map/ppermute | solution.py:372
  69.9 4.5 %collective-permute-start.20 = (bf16[128,256]{1,0:T(8,128)(2,1)S(1)}, bf16[128,256]{1,0:T(8,128)(2,1)S(1)}, u32[]{:S(2)}, u32[]{:S(2)}) collective-permute-start(bf16[128,256]{1,0:T(8,128)(2,1)S(1)} %shard_map.145.refs_0_), channel_id=1, source_target_pairs={{0,4},{1,5},{2,6},{3,7},{4,0},{5,1},{6,2},{7,3},{8,12},{9,13},{10,... | collective-permute-start | bytes 196616 | tf_op jit(solution)/shard_map/ppermute | solution.py:372
  73.0 7.7 %collective-permute-start.24 = (bf16[128,256]{1,0:T(8,128)(2,1)S(1)}, bf16[128,256]{1,0:T(8,128)(2,1)S(1)}, u32[]{:S(2)}, u32[]{:S(2)}) collective-permute-start(bf16[128,256]{1,0:T(8,128)(2,1)S(1)} %shard_map.145.refs_0_), channel_id=1, source_target_pairs={{0,2},{1,3},{2,0},{3,1},{4,6},{5,7},{6,4},{7,5},{8,10},{9,11},{10,... | collective-permute-start | bytes 196616 | tf_op jit(solution)/shard_map/ppermute | solution.py:372
  74.4 6.3 %collective-permute-start.27 = (bf16[128,256]{1,0:T(8,128)(2,1)S(1)}, bf16[128,256]{1,0:T(8,128)(2,1)S(1)}, u32[]{:S(2)}, u32[]{:S(2)}) collective-permute-start(bf16[128,256]{1,0:T(8,128)(2,1)S(1)} %collective-permute-done.22.refs_3_), channel_id=1, source_target_pairs={{0,2},{1,3},{2,0},{3,1},{4,6},{5,7},{6,4},{7,5},{8,10},{9,11},{10,... | collective-permute-start | bytes 196616 | tf_op jit(solution)/shard_map/ppermute | solution.py:372
  75.7 5.0 %collective-permute-start.26 = (bf16[128,256]{1,0:T(8,128)(2,1)S(1)}, bf16[128,256]{1,0:T(8,128)(2,1)S(1)}, u32[]{:S(2)}, u32[]{:S(2)}) collective-permute-start(bf16[128,256]{1,0:T(8,128)(2,1)S(1)} %collective-permute-done.21.refs_2_), channel_id=1, source_target_pairs={{0,2},{1,3},{2,0},{3,1},{4,6},{5,7},{6,4},{7,5},{8,10},{9,11},{10,... | collective-permute-start | bytes 196616 | tf_op jit(solution)/shard_map/ppermute | solution.py:372
  76.4 4.3 %collective-permute-start.25 = (bf16[128,256]{1,0:T(8,128)(2,1)S(1)}, bf16[128,256]{1,0:T(8,128)(2,1)S(1)}, u32[]{:S(2)}, u32[]{:S(2)}) collective-permute-start(bf16[128,256]{1,0:T(8,128)(2,1)S(1)} %collective-permute-done.20.refs_1_), channel_id=1, source_target_pairs={{0,2},{1,3},{2,0},{3,1},{4,6},{5,7},{6,4},{7,5},{8,10},{9,11},{10,... | collective-permute-start | bytes 196616 | tf_op jit(solution)/shard_map/ppermute | solution.py:372
  86.3 5.4 %collective-permute-start.28 = (bf16[2,16,2048]{2,1,0:T(8,128)(2,1)S(1)}, bf16[2,16,2048]{2,1,0:T(8,128)(2,1)S(1)}, u32[]{:S(2)}, u32[]{:S(2)}) collective-permute-start(bf16[2,16,2048]{2,1,0:T(8,128)(2,1)S(1)} %get-tuple-element.33), channel_id=1, source_target_pairs={{0,2},{1,3},{2,0},{3,1},{4,6},{5,7},{6,4},{7,5},{8,10},{9,11},{10,... | collective-permute-start | bytes 393224 | tf_op jit(solution)/shard_map/ppermute | solution.py:372
  87.6 7.1 %collective-permute-start.31 = (bf16[2,16,2048]{2,1,0:T(8,128)(2,1)S(1)}, bf16[2,16,2048]{2,1,0:T(8,128)(2,1)S(1)}, u32[]{:S(2)}, u32[]{:S(2)}) collective-permute-start(bf16[2,16,2048]{2,1,0:T(8,128)(2,1)S(1)} %get-tuple-element.37), channel_id=1, source_target_pairs={{0,2},{1,3},{2,0},{3,1},{4,6},{5,7},{6,4},{7,5},{8,10},{9,11},{10,... | collective-permute-start | bytes 393224 | tf_op jit(solution)/shard_map/ppermute | solution.py:372
  91.7 6.1 %collective-permute-start.29 = (bf16[16,2048]{1,0:T(8,128)(2,1)S(1)}, bf16[16,2048]{1,0:T(8,128)(2,1)S(1)}, u32[]{:S(2)}, u32[]{:S(2)}) collective-permute-start(bf16[16,2048]{1,0:T(8,128)(2,1)S(1)} %get-tuple-element.34), channel_id=1, source_target_pairs={{0,12},{1,13},{2,14},{3,15},{4,8},{5,9},{6,10},{7,11},{8,4},{9,5},... | collective-permute-start | bytes 196616 | tf_op jit(solution)/shard_map/ppermute | solution.py:372
  94.6 5.4 %collective-permute-start.30 = (bf16[16,2048]{1,0:T(8,128)(2,1)S(1)}, bf16[16,2048]{1,0:T(8,128)(2,1)S(1)}, u32[]{:S(2)}, u32[]{:S(2)}) collective-permute-start(bf16[16,2048]{1,0:T(8,128)(2,1)S(1)} %get-tuple-element.35), channel_id=1, source_target_pairs={{0,8},{1,9},{2,10},{3,11},{4,12},{5,13},{6,14},{7,15},{8,0},{9,1},... | collective-permute-start | bytes 196616 | tf_op jit(solution)/shard_map/ppermute | solution.py:372
  94.7 5.3 %collective-permute-start.32 = (bf16[16,2048]{1,0:T(8,128)(2,1)S(1)}, bf16[16,2048]{1,0:T(8,128)(2,1)S(1)}, u32[]{:S(2)}, u32[]{:S(2)}) collective-permute-start(bf16[16,2048]{1,0:T(8,128)(2,1)S(1)} %get-tuple-element.38), channel_id=1, source_target_pairs={{0,4},{1,5},{2,6},{3,7},{4,0},{5,1},{6,2},{7,3},{8,12},{9,13},{10,... | collective-permute-start | bytes 196616 | tf_op jit(solution)/shard_map/ppermute | solution.py:372
  (12 other events, 63.6 us)
